TPU v7x, 256 devices: a whole 4x4x8 slice. The times are simulated.
256 devices in a mesh: section: 8 (over x_lo, y), expert: 32 (over z, x_hi, core).
Axes of the slice: x: 4 (x_hi: 2, x_lo: 2; x = x_hi * 2 + x_lo), y: 4, z: 8, core: 2. Of those that a mesh axis runs over, the one named last changes fastest.
Arguments:
- tokens: bfloat16 [8, 512, 2048], P('section', 'expert'), may hold values from -12 to 12
- expert_ids: int32 [2, 8, 8, 512, 6], P(None, 'section', None, 'expert'), may hold values from 0 to 63, all different within a row; in each aligned block of 16 rows (0 to 15, 16 to 31, ..., all dimensions but the last counted through in order) at most 2 rows name the same one
- norm_gain: float32 [2, 8, 2048], P(None, 'section'), may hold values from 0.5 to 1.5
- router_weight: bfloat16 [2, 8, 2048, 64], P(None, 'section'), may hold values from -0.125 to 0.125
- gate_weight: bfloat16 [2, 8, 32, 2048, 384], P(None, 'section', 'expert'), may hold values from -0.125 to 0.125
- up_weight: bfloat16 [2, 8, 32, 2048, 384], P(None, 'section', 'expert'), may hold values from -0.125 to 0.125
- down_weight: bfloat16 [2, 8, 32, 384, 2048], P(None, 'section', 'expert'), may hold values from -0.4375 to 0.4375
Outputs:
- window_output: bfloat16 [8, 512, 2048], P('section', 'expert')
Inputs may be any that keep to these rules, and one draw needn't show every extreme that they name: `expert_ids`: each row names 6 different experts. Within the 16 rows of one device for one layer and one microbatch, no expert is named by more than 2 rows, and in some such block one expert is named by exactly 2 rows.
All inputs are finite; a program needn't handle non-finite values.
Results may differ from a plain program's by a relative error of at most 0.02.
Values may be sent and summed in bfloat16 or wider, within the bound.
A program may use at most 64 MiB of HBM per device.

v0:
```python
import jax
import jax.numpy as jnp
from jax import lax
from jax.sharding import PartitionSpec as P

CAP = 2


norm_epsilon = 1e-06


def from_behind(block, axis, distance):
    devices = range(lax.axis_size(axis))
    route = [((i - distance) % len(devices), i) for i in devices]
    return lax.ppermute(block, axis, route)


def passed_along(value, axis, steps):
    count = lax.axis_size(axis)
    initial, last = (max(0, -steps), min(count, count - steps))
    return lax.ppermute(value, axis, [(source, source + steps) for source in range(initial, last)])


def expert_rows(rows_in, gate_piece, up_piece, down_piece):
    rows_flat = rows_in.reshape(-1, rows_in.shape[-1])
    gate_act = jnp.dot(rows_flat, gate_piece, preferred_element_type=jnp.float32)
    up_act = jnp.dot(rows_flat, up_piece, preferred_element_type=jnp.float32)
    hidden = (jax.nn.silu(gate_act) * up_act).astype(jnp.bfloat16)
    partial_out = jnp.dot(hidden, down_piece, preferred_element_type=jnp.float32).astype(
        jnp.bfloat16
    )
    return partial_out.reshape(rows_in.shape[:-1] + (down_piece.shape[1],))


def route_slots(ids_now, held_count):
    onehot = (ids_now[:, :, None] == jnp.arange(held_count, dtype=jnp.int32)).astype(jnp.int32)
    pairs = onehot.reshape(-1, held_count)
    rank_in = jnp.cumsum(pairs, axis=0) - pairs
    slot_of = jnp.sum(rank_in * pairs, axis=1).reshape(ids_now.shape)
    return jnp.where(ids_now < held_count, ids_now * CAP + slot_of, held_count * CAP)


def moe_layer(current, ids_now, gain_row, router_now, gate_piece, up_piece, down_piece):
    stream = current.astype(jnp.float32)
    features = stream.shape[1]
    mean_square = jnp.mean(stream * stream, axis=-1, keepdims=True)
    normed = (stream * lax.rsqrt(mean_square + norm_epsilon) * gain_row).astype(jnp.bfloat16)
    logits = jnp.dot(normed, router_now, preferred_element_type=jnp.float32)
    picked = jnp.take_along_axis(logits, ids_now, axis=1)
    scores = jax.nn.sigmoid(picked)
    gate_share = scores / jnp.sum(scores, axis=1, keepdims=True)
    held_count = lax.axis_size("expert") // 2
    position = route_slots(ids_now, held_count)
    select = position[None, :, :] == jnp.arange(held_count * CAP, dtype=jnp.int32)[:, None, None]
    choose = jnp.sum(select.astype(jnp.float32), axis=2).astype(jnp.bfloat16)
    outgoing = jnp.dot(choose, normed, preferred_element_type=jnp.float32).astype(jnp.bfloat16)
    outgoing = outgoing.reshape(held_count, CAP, features)
    partial_out = expert_rows(
        lax.all_to_all(
            jnp.repeat(outgoing, 2, axis=0), "expert", split_axis=0, concat_axis=0, tiled=True
        ),
        gate_piece,
        up_piece,
        down_piece,
    )
    returned = lax.all_to_all(partial_out, "expert", split_axis=0, concat_axis=0, tiled=True)
    summed = returned.reshape(held_count, 2, CAP, features).astype(jnp.float32).sum(axis=1)
    expert_out = summed.astype(jnp.bfloat16)
    expert_out = lax.optimization_barrier(expert_out).astype(jnp.float32)
    padded = jnp.concatenate(
        [expert_out.reshape(held_count * CAP, features), jnp.zeros((1, features), jnp.float32)],
        axis=0,
    )
    values = padded[position]
    branch_sum = jnp.sum(gate_share[:, :, None] * values, axis=1)
    return (stream + branch_sum).astype(jnp.bfloat16)


def body(tokens, expert_ids, norm_gain, router_weight, gate_weight, up_weight, down_weight):
    sections = lax.axis_size("section")
    section_index = lax.axis_index("section")
    id_table = expert_ids[:, 0]
    gain_table = norm_gain[:, 0]
    router_table = router_weight[:, 0]
    gate_table = gate_weight[:, 0, 0]
    up_table = up_weight[:, 0, 0]
    down_table = down_weight[:, 0, 0]
    row_count = id_table.shape[2]
    top_count = id_table.shape[3]

    def tick(step_index, carried, returning, move_back):
        offset = step_index - section_index
        virtual = jnp.clip(offset // sections, 0, 1)
        micro = jnp.clip(offset - virtual * sections, 0, sections - 1)
        inject = (section_index == 0) & (step_index < sections)
        current = jnp.where(inject, returning, carried)
        ids_now = lax.dynamic_slice(
            id_table, (virtual, micro, 0, 0), (1, 1, row_count, top_count)
        ).reshape(row_count, top_count)

        def layer_of(table):
            return lax.dynamic_index_in_dim(table, virtual, 0, keepdims=False)

        result = moe_layer(
            current,
            ids_now,
            layer_of(gain_table),
            layer_of(router_table),
            layer_of(gate_table),
            layer_of(up_table),
            layer_of(down_table),
        )
        finished = (section_index == sections - 1) & (offset >= sections) & (offset < 2 * sections)
        returning = jnp.where(finished, result, returning)
        carried = from_behind(result, "section", 1)
        if move_back:
            returning = passed_along(returning, "section", -1)
        return (carried, returning)

    start_state = (jnp.zeros_like(tokens[0]), tokens[0])
    carried, returning = lax.fori_loop(
        0,
        3 * sections - 2,
        lambda step_index, state: tick(step_index, state[0], state[1], True),
        start_state,
    )
    carried, returning = tick(3 * sections - 2, carried, returning, False)
    return returning[None]


def solution(mesh):
    return jax.shard_map(
        body,
        mesh=mesh,
        in_specs=(
            P("section", "expert", None),
            P(None, "section", None, "expert", None),
            P(None, "section", None),
            P(None, "section", None, None),
            P(None, "section", "expert", None, None),
            P(None, "section", "expert", None, None),
            P(None, "section", "expert", None, None),
        ),
        out_specs=P("section", "expert", None),
        check_vma=False,
    )
```

profile of v0, /device:TPU:26, one launch (start us, length us, event | category | flops | bytes accessed | tf_op | source)
XLA Modules:
  0.0 1326.2 jit_solution(9159512734179292114)
XLA Ops:
  7.3 1267.9 %while.17 = (s32[]{:T(128)}, bf16[16,2048]{1,0:T(8,128)(2,1)S(1)}, bf16[16,2048]{1,0:T(8,128)(2,1)S(1)}, pred[]{:T(512)}, s32[]{:T(128)}, /*index=5*/f32[2,2048]...) while((s32[]{:T(128)}, bf16[16,2048]{1,0:T(8,128)(2,1)S(1)}, ...), condition=%wide.region_8.10_spmd, body=%wide.region_0.9_spmd.sunk | while | flops 309813536 | bytes 28671900 | solution.py:121
  11.7 10.5 all-to-all-start
  23.7 11.6 all-to-all-done
  50.3 10.5 all-to-all-done.1
  78.9 11.6 all-to-all-done
  105.4 10.5 all-to-all-done.1
  134.4 11.6 all-to-all-done
  160.9 10.5 all-to-all-done.1
  191.4 11.6 all-to-all-done
  218.0 10.5 all-to-all-done.1
  248.7 11.6 all-to-all-done
  275.2 10.5 all-to-all-done.1
  287.4 5.2 collective-permute-start
  306.3 11.6 all-to-all-done
  332.8 10.5 all-to-all-done.1
  345.1 5.2 collective-permute-start
  363.9 11.6 all-to-all-done
  390.4 10.5 all-to-all-done.1
  402.7 5.2 collective-permute-start
  421.5 11.6 all-to-all-done
  448.0 10.5 all-to-all-done.1
  460.3 5.2 collective-permute-start
  479.1 11.6 all-to-all-done
  505.6 10.5 all-to-all-done.1
  517.9 5.2 collective-permute-start
  536.7 11.6 all-to-all-done
  563.2 10.5 all-to-all-done.1
  575.5 5.2 collective-permute-start
  594.3 11.6 all-to-all-done
  620.8 10.5 all-to-all-done.1
  633.1 5.2 collective-permute-start
  651.9 11.6 all-to-all-done
  678.5 10.5 all-to-all-done.1
  709.6 11.6 all-to-all-done
  736.1 10.5 all-to-all-done.1
  748.3 5.2 collective-permute-start
  767.2 11.6 all-to-all-done
  793.7 10.5 all-to-all-done.1
  824.8 11.6 all-to-all-done
  851.3 10.5 all-to-all-done.1
  863.6 5.2 collective-permute-start
  882.4 11.6 all-to-all-done
  908.9 10.5 all-to-all-done.1
  921.2 5.2 collective-permute-start
  940.0 11.6 all-to-all-done
  966.5 10.5 all-to-all-done.1
  978.8 5.2 collective-permute-start
  997.6 11.6 all-to-all-done
  1024.1 10.5 all-to-all-done.1
  1036.4 5.2 collective-permute-start
  1055.2 11.6 all-to-all-done
  1081.7 10.5 all-to-all-done.1
  1094.0 5.2 collective-permute-start
  1112.8 11.6 all-to-all-done
  1139.4 10.5 all-to-all-done.1
  1151.6 5.2 collective-permute-start
  1170.5 11.6 all-to-all-done
  1197.0 10.5 all-to-all-done.1
  1209.2 5.2 collective-permute-start
  1228.1 11.6 all-to-all-done
  1254.6 10.5 all-to-all-done.1
  1266.9 5.2 collective-permute-start
  1286.5 11.6 all-to-all-done.2
  1312.6 11.1 all-to-all-done.3
  (1178 shorter events, 721.4 us)
Async XLA Ops:
  11.7 23.6 %all-to-all-start = ((bf16[32,2,2048]{2,1,0:T(2,128)(2,1)}), bf16[32,2,2048]{2,1,0:T(2,128)(2,1)}, u32[]{:S(2)}, u32[]{:S(2)}) async-start(bf16[32,2,2048]{2,1,0:T(2,128)(2,1)} %bitcast.172), calls=%async_computation | async-start | bytes 524288 | tf_op jit(solution)/shard_map/while/body/eval_jaxpr/all_to_all | solution.py:59
  43.7 17.1 %all-to-all-start.1 = ((bf16[32,2,2048]{2,1,0:T(2,128)(2,1)}), bf16[32,2,2048]{2,1,0:T(2,128)(2,1)S(1)}, u32[]{:S(2)}, u32[]{:S(2)}) async-start(bf16[32,2,2048]{2,1,0:T(2,128)(2,1)} %reshape.392), calls=%async_computation.1 | async-start | bytes 524288 | tf_op jit(solution)/shard_map/while/body/eval_jaxpr/all_to_all | solution.py:66
  72.8 17.6 %all-to-all-start = ((bf16[32,2,2048]{2,1,0:T(2,128)(2,1)}), bf16[32,2,2048]{2,1,0:T(2,128)(2,1)}, u32[]{:S(2)}, u32[]{:S(2)}) async-start(bf16[32,2,2048]{2,1,0:T(2,128)(2,1)} %bitcast.172), calls=%async_computation | async-start | bytes 524288 | tf_op jit(solution)/shard_map/while/body/eval_jaxpr/all_to_all | solution.py:59
  98.8 17.1 %all-to-all-start.1 = ((bf16[32,2,2048]{2,1,0:T(2,128)(2,1)}), bf16[32,2,2048]{2,1,0:T(2,128)(2,1)S(1)}, u32[]{:S(2)}, u32[]{:S(2)}) async-start(bf16[32,2,2048]{2,1,0:T(2,128)(2,1)} %reshape.392), calls=%async_computation.1 | async-start | bytes 524288 | tf_op jit(solution)/shard_map/while/body/eval_jaxpr/all_to_all | solution.py:66
  128.3 17.6 %all-to-all-start = ((bf16[32,2,2048]{2,1,0:T(2,128)(2,1)}), bf16[32,2,2048]{2,1,0:T(2,128)(2,1)}, u32[]{:S(2)}, u32[]{:S(2)}) async-start(bf16[32,2,2048]{2,1,0:T(2,128)(2,1)} %bitcast.172), calls=%async_computation | async-start | bytes 524288 | tf_op jit(solution)/shard_map/while/body/eval_jaxpr/all_to_all | solution.py:59
  154.3 17.1 %all-to-all-start.1 = ((bf16[32,2,2048]{2,1,0:T(2,128)(2,1)}), bf16[32,2,2048]{2,1,0:T(2,128)(2,1)S(1)}, u32[]{:S(2)}, u32[]{:S(2)}) async-start(bf16[32,2,2048]{2,1,0:T(2,128)(2,1)} %reshape.392), calls=%async_computation.1 | async-start | bytes 524288 | tf_op jit(solution)/shard_map/while/body/eval_jaxpr/all_to_all | solution.py:66
  185.4 17.6 %all-to-all-start = ((bf16[32,2,2048]{2,1,0:T(2,128)(2,1)}), bf16[32,2,2048]{2,1,0:T(2,128)(2,1)}, u32[]{:S(2)}, u32[]{:S(2)}) async-start(bf16[32,2,2048]{2,1,0:T(2,128)(2,1)} %bitcast.172), calls=%async_computation | async-start | bytes 524288 | tf_op jit(solution)/shard_map/while/body/eval_jaxpr/all_to_all | solution.py:59
  211.3 17.1 %all-to-all-start.1 = ((bf16[32,2,2048]{2,1,0:T(2,128)(2,1)}), bf16[32,2,2048]{2,1,0:T(2,128)(2,1)S(1)}, u32[]{:S(2)}, u32[]{:S(2)}) async-start(bf16[32,2,2048]{2,1,0:T(2,128)(2,1)} %reshape.392), calls=%async_computation.1 | async-start | bytes 524288 | tf_op jit(solution)/shard_map/while/body/eval_jaxpr/all_to_all | solution.py:66
  242.6 17.6 %all-to-all-start = ((bf16[32,2,2048]{2,1,0:T(2,128)(2,1)}), bf16[32,2,2048]{2,1,0:T(2,128)(2,1)}, u32[]{:S(2)}, u32[]{:S(2)}) async-start(bf16[32,2,2048]{2,1,0:T(2,128)(2,1)} %bitcast.172), calls=%async_computation | async-start | bytes 524288 | tf_op jit(solution)/shard_map/while/body/eval_jaxpr/all_to_all | solution.py:59
  268.5 17.1 %all-to-all-start.1 = ((bf16[32,2,2048]{2,1,0:T(2,128)(2,1)}), bf16[32,2,2048]{2,1,0:T(2,128)(2,1)S(1)}, u32[]{:S(2)}, u32[]{:S(2)}) async-start(bf16[32,2,2048]{2,1,0:T(2,128)(2,1)} %reshape.392), calls=%async_computation.1 | async-start | bytes 524288 | tf_op jit(solution)/shard_map/while/body/eval_jaxpr/all_to_all | solution.py:66
  287.4 7.1 collective-permute-start
  300.2 17.6 %all-to-all-start = ((bf16[32,2,2048]{2,1,0:T(2,128)(2,1)}), bf16[32,2,2048]{2,1,0:T(2,128)(2,1)}, u32[]{:S(2)}, u32[]{:S(2)}) async-start(bf16[32,2,2048]{2,1,0:T(2,128)(2,1)} %bitcast.172), calls=%async_computation | async-start | bytes 524288 | tf_op jit(solution)/shard_map/while/body/eval_jaxpr/all_to_all | solution.py:59
  326.1 17.1 %all-to-all-start.1 = ((bf16[32,2,2048]{2,1,0:T(2,128)(2,1)}), bf16[32,2,2048]{2,1,0:T(2,128)(2,1)S(1)}, u32[]{:S(2)}, u32[]{:S(2)}) async-start(bf16[32,2,2048]{2,1,0:T(2,128)(2,1)} %reshape.392), calls=%async_computation.1 | async-start | bytes 524288 | tf_op jit(solution)/shard_map/while/body/eval_jaxpr/all_to_all | solution.py:66
  345.1 7.1 collective-permute-start
  357.8 17.6 %all-to-all-start = ((bf16[32,2,2048]{2,1,0:T(2,128)(2,1)}), bf16[32,2,2048]{2,1,0:T(2,128)(2,1)}, u32[]{:S(2)}, u32[]{:S(2)}) async-start(bf16[32,2,2048]{2,1,0:T(2,128)(2,1)} %bitcast.172), calls=%async_computation | async-start | bytes 524288 | tf_op jit(solution)/shard_map/while/body/eval_jaxpr/all_to_all | solution.py:59
  383.7 17.1 %all-to-all-start.1 = ((bf16[32,2,2048]{2,1,0:T(2,128)(2,1)}), bf16[32,2,2048]{2,1,0:T(2,128)(2,1)S(1)}, u32[]{:S(2)}, u32[]{:S(2)}) async-start(bf16[32,2,2048]{2,1,0:T(2,128)(2,1)} %reshape.392), calls=%async_computation.1 | async-start | bytes 524288 | tf_op jit(solution)/shard_map/while/body/eval_jaxpr/all_to_all | solution.py:66
  402.7 7.1 collective-permute-start
  415.4 17.6 %all-to-all-start = ((bf16[32,2,2048]{2,1,0:T(2,128)(2,1)}), bf16[32,2,2048]{2,1,0:T(2,128)(2,1)}, u32[]{:S(2)}, u32[]{:S(2)}) async-start(bf16[32,2,2048]{2,1,0:T(2,128)(2,1)} %bitcast.172), calls=%async_computation | async-start | bytes 524288 | tf_op jit(solution)/shard_map/while/body/eval_jaxpr/all_to_all | solution.py:59
  441.4 17.1 %all-to-all-start.1 = ((bf16[32,2,2048]{2,1,0:T(2,128)(2,1)}), bf16[32,2,2048]{2,1,0:T(2,128)(2,1)S(1)}, u32[]{:S(2)}, u32[]{:S(2)}) async-start(bf16[32,2,2048]{2,1,0:T(2,128)(2,1)} %reshape.392), calls=%async_computation.1 | async-start | bytes 524288 | tf_op jit(solution)/shard_map/while/body/eval_jaxpr/all_to_all | solution.py:66
  460.3 7.1 collective-permute-start
  473.1 17.6 %all-to-all-start = ((bf16[32,2,2048]{2,1,0:T(2,128)(2,1)}), bf16[32,2,2048]{2,1,0:T(2,128)(2,1)}, u32[]{:S(2)}, u32[]{:S(2)}) async-start(bf16[32,2,2048]{2,1,0:T(2,128)(2,1)} %bitcast.172), calls=%async_computation | async-start | bytes 524288 | tf_op jit(solution)/shard_map/while/body/eval_jaxpr/all_to_all | solution.py:59
  499.0 17.1 %all-to-all-start.1 = ((bf16[32,2,2048]{2,1,0:T(2,128)(2,1)}), bf16[32,2,2048]{2,1,0:T(2,128)(2,1)S(1)}, u32[]{:S(2)}, u32[]{:S(2)}) async-start(bf16[32,2,2048]{2,1,0:T(2,128)(2,1)} %reshape.392), calls=%async_computation.1 | async-start | bytes 524288 | tf_op jit(solution)/shard_map/while/body/eval_jaxpr/all_to_all | solution.py:66
  517.9 7.1 collective-permute-start
  530.7 17.6 %all-to-all-start = ((bf16[32,2,2048]{2,1,0:T(2,128)(2,1)}), bf16[32,2,2048]{2,1,0:T(2,128)(2,1)}, u32[]{:S(2)}, u32[]{:S(2)}) async-start(bf16[32,2,2048]{2,1,0:T(2,128)(2,1)} %bitcast.172), calls=%async_computation | async-start | bytes 524288 | tf_op jit(solution)/shard_map/while/body/eval_jaxpr/all_to_all | solution.py:59
  556.6 17.1 %all-to-all-start.1 = ((bf16[32,2,2048]{2,1,0:T(2,128)(2,1)}), bf16[32,2,2048]{2,1,0:T(2,128)(2,1)S(1)}, u32[]{:S(2)}, u32[]{:S(2)}) async-start(bf16[32,2,2048]{2,1,0:T(2,128)(2,1)} %reshape.392), calls=%async_computation.1 | async-start | bytes 524288 | tf_op jit(solution)/shard_map/while/body/eval_jaxpr/all_to_all | solution.py:66
  575.5 7.1 collective-permute-start
  588.3 17.6 %all-to-all-start = ((bf16[32,2,2048]{2,1,0:T(2,128)(2,1)}), bf16[32,2,2048]{2,1,0:T(2,128)(2,1)}, u32[]{:S(2)}, u32[]{:S(2)}) async-start(bf16[32,2,2048]{2,1,0:T(2,128)(2,1)} %bitcast.172), calls=%async_computation | async-start | bytes 524288 | tf_op jit(solution)/shard_map/while/body/eval_jaxpr/all_to_all | solution.py:59
  614.2 17.1 %all-to-all-start.1 = ((bf16[32,2,2048]{2,1,0:T(2,128)(2,1)}), bf16[32,2,2048]{2,1,0:T(2,128)(2,1)S(1)}, u32[]{:S(2)}, u32[]{:S(2)}) async-start(bf16[32,2,2048]{2,1,0:T(2,128)(2,1)} %reshape.392), calls=%async_computation.1 | async-start | bytes 524288 | tf_op jit(solution)/shard_map/while/body/eval_jaxpr/all_to_all | solution.py:66
  633.1 7.1 collective-permute-start
  645.9 17.6 %all-to-all-start = ((bf16[32,2,2048]{2,1,0:T(2,128)(2,1)}), bf16[32,2,2048]{2,1,0:T(2,128)(2,1)}, u32[]{:S(2)}, u32[]{:S(2)}) async-start(bf16[32,2,2048]{2,1,0:T(2,128)(2,1)} %bitcast.172), calls=%async_computation | async-start | bytes 524288 | tf_op jit(solution)/shard_map/while/body/eval_jaxpr/all_to_all | solution.py:59
  671.8 17.1 %all-to-all-start.1 = ((bf16[32,2,2048]{2,1,0:T(2,128)(2,1)}), bf16[32,2,2048]{2,1,0:T(2,128)(2,1)S(1)}, u32[]{:S(2)}, u32[]{:S(2)}) async-start(bf16[32,2,2048]{2,1,0:T(2,128)(2,1)} %reshape.392), calls=%async_computation.1 | async-start | bytes 524288 | tf_op jit(solution)/shard_map/while/body/eval_jaxpr/all_to_all | solution.py:66
  690.7 7.1 collective-permute-start
  703.5 17.6 %all-to-all-start = ((bf16[32,2,2048]{2,1,0:T(2,128)(2,1)}), bf16[32,2,2048]{2,1,0:T(2,128)(2,1)}, u32[]{:S(2)}, u32[]{:S(2)}) async-start(bf16[32,2,2048]{2,1,0:T(2,128)(2,1)} %bitcast.172), calls=%async_computation | async-start | bytes 524288 | tf_op jit(solution)/shard_map/while/body/eval_jaxpr/all_to_all | solution.py:59
  729.4 17.1 %all-to-all-start.1 = ((bf16[32,2,2048]{2,1,0:T(2,128)(2,1)}), bf16[32,2,2048]{2,1,0:T(2,128)(2,1)S(1)}, u32[]{:S(2)}, u32[]{:S(2)}) async-start(bf16[32,2,2048]{2,1,0:T(2,128)(2,1)} %reshape.392), calls=%async_computation.1 | async-start | bytes 524288 | tf_op jit(solution)/shard_map/while/body/eval_jaxpr/all_to_all | solution.py:66
  748.3 7.1 collective-permute-start
  761.1 17.6 %all-to-all-start = ((bf16[32,2,2048]{2,1,0:T(2,128)(2,1)}), bf16[32,2,2048]{2,1,0:T(2,128)(2,1)}, u32[]{:S(2)}, u32[]{:S(2)}) async-start(bf16[32,2,2048]{2,1,0:T(2,128)(2,1)} %bitcast.172), calls=%async_computation | async-start | bytes 524288 | tf_op jit(solution)/shard_map/while/body/eval_jaxpr/all_to_all | solution.py:59
  787.0 17.1 %all-to-all-start.1 = ((bf16[32,2,2048]{2,1,0:T(2,128)(2,1)}), bf16[32,2,2048]{2,1,0:T(2,128)(2,1)S(1)}, u32[]{:S(2)}, u32[]{:S(2)}) async-start(bf16[32,2,2048]{2,1,0:T(2,128)(2,1)} %reshape.392), calls=%async_computation.1 | async-start | bytes 524288 | tf_op jit(solution)/shard_map/while/body/eval_jaxpr/all_to_all | solution.py:66
  806.0 7.1 collective-permute-start
  818.7 17.6 %all-to-all-start = ((bf16[32,2,2048]{2,1,0:T(2,128)(2,1)}), bf16[32,2,2048]{2,1,0:T(2,128)(2,1)}, u32[]{:S(2)}, u32[]{:S(2)}) async-start(bf16[32,2,2048]{2,1,0:T(2,128)(2,1)} %bitcast.172), calls=%async_computation | async-start | bytes 524288 | tf_op jit(solution)/shard_map/while/body/eval_jaxpr/all_to_all | solution.py:59
  844.6 17.1 %all-to-all-start.1 = ((bf16[32,2,2048]{2,1,0:T(2,128)(2,1)}), bf16[32,2,2048]{2,1,0:T(2,128)(2,1)S(1)}, u32[]{:S(2)}, u32[]{:S(2)}) async-start(bf16[32,2,2048]{2,1,0:T(2,128)(2,1)} %reshape.392), calls=%async_computation.1 | async-start | bytes 524288 | tf_op jit(solution)/shard_map/while/body/eval_jaxpr/all_to_all | solution.py:66
  863.6 7.1 collective-permute-start
  876.3 17.6 %all-to-all-start = ((bf16[32,2,2048]{2,1,0:T(2,128)(2,1)}), bf16[32,2,2048]{2,1,0:T(2,128)(2,1)}, u32[]{:S(2)}, u32[]{:S(2)}) async-start(bf16[32,2,2048]{2,1,0:T(2,128)(2,1)} %bitcast.172), calls=%async_computation | async-start | bytes 524288 | tf_op jit(solution)/shard_map/while/body/eval_jaxpr/all_to_all | solution.py:59
  902.3 17.1 %all-to-all-start.1 = ((bf16[32,2,2048]{2,1,0:T(2,128)(2,1)}), bf16[32,2,2048]{2,1,0:T(2,128)(2,1)S(1)}, u32[]{:S(2)}, u32[]{:S(2)}) async-start(bf16[32,2,2048]{2,1,0:T(2,128)(2,1)} %reshape.392), calls=%async_computation.1 | async-start | bytes 524288 | tf_op jit(solution)/shard_map/while/body/eval_jaxpr/all_to_all | solution.py:66
  921.2 7.1 collective-permute-start
  934.0 17.6 %all-to-all-start = ((bf16[32,2,2048]{2,1,0:T(2,128)(2,1)}), bf16[32,2,2048]{2,1,0:T(2,128)(2,1)}, u32[]{:S(2)}, u32[]{:S(2)}) async-start(bf16[32,2,2048]{2,1,0:T(2,128)(2,1)} %bitcast.172), calls=%async_computation | async-start | bytes 524288 | tf_op jit(solution)/shard_map/while/body/eval_jaxpr/all_to_all | solution.py:59
  959.9 17.1 %all-to-all-start.1 = ((bf16[32,2,2048]{2,1,0:T(2,128)(2,1)}), bf16[32,2,2048]{2,1,0:T(2,128)(2,1)S(1)}, u32[]{:S(2)}, u32[]{:S(2)}) async-start(bf16[32,2,2048]{2,1,0:T(2,128)(2,1)} %reshape.392), calls=%async_computation.1 | async-start | bytes 524288 | tf_op jit(solution)/shard_map/while/body/eval_jaxpr/all_to_all | solution.py:66
  978.8 7.1 collective-permute-start
  991.6 17.6 %all-to-all-start = ((bf16[32,2,2048]{2,1,0:T(2,128)(2,1)}), bf16[32,2,2048]{2,1,0:T(2,128)(2,1)}, u32[]{:S(2)}, u32[]{:S(2)}) async-start(bf16[32,2,2048]{2,1,0:T(2,128)(2,1)} %bitcast.172), calls=%async_computation | async-start | bytes 524288 | tf_op jit(solution)/shard_map/while/body/eval_jaxpr/all_to_all | solution.py:59
  1017.5 17.1 %all-to-all-start.1 = ((bf16[32,2,2048]{2,1,0:T(2,128)(2,1)}), bf16[32,2,2048]{2,1,0:T(2,128)(2,1)S(1)}, u32[]{:S(2)}, u32[]{:S(2)}) async-start(bf16[32,2,2048]{2,1,0:T(2,128)(2,1)} %reshape.392), calls=%async_computation.1 | async-start | bytes 524288 | tf_op jit(solution)/shard_map/while/body/eval_jaxpr/all_to_all | solution.py:66
  1036.4 7.1 collective-permute-start
  1049.2 17.6 %all-to-all-start = ((bf16[32,2,2048]{2,1,0:T(2,128)(2,1)}), bf16[32,2,2048]{2,1,0:T(2,128)(2,1)}, u32[]{:S(2)}, u32[]{:S(2)}) async-start(bf16[32,2,2048]{2,1,0:T(2,128)(2,1)} %bitcast.172), calls=%async_computation | async-start | bytes 524288 | tf_op jit(solution)/shard_map/while/body/eval_jaxpr/all_to_all | solution.py:59
  1075.1 17.1 %all-to-all-start.1 = ((bf16[32,2,2048]{2,1,0:T(2,128)(2,1)}), bf16[32,2,2048]{2,1,0:T(2,128)(2,1)S(1)}, u32[]{:S(2)}, u32[]{:S(2)}) async-start(bf16[32,2,2048]{2,1,0:T(2,128)(2,1)} %reshape.392), calls=%async_computation.1 | async-start | bytes 524288 | tf_op jit(solution)/shard_map/while/body/eval_jaxpr/all_to_all | solution.py:66
  1094.0 7.1 collective-permute-start
  1106.8 17.6 %all-to-all-start = ((bf16[32,2,2048]{2,1,0:T(2,128)(2,1)}), bf16[32,2,2048]{2,1,0:T(2,128)(2,1)}, u32[]{:S(2)}, u32[]{:S(2)}) async-start(bf16[32,2,2048]{2,1,0:T(2,128)(2,1)} %bitcast.172), calls=%async_computation | async-start | bytes 524288 | tf_op jit(solution)/shard_map/while/body/eval_jaxpr/all_to_all | solution.py:59
  1132.7 17.1 %all-to-all-start.1 = ((bf16[32,2,2048]{2,1,0:T(2,128)(2,1)}), bf16[32,2,2048]{2,1,0:T(2,128)(2,1)S(1)}, u32[]{:S(2)}, u32[]{:S(2)}) async-start(bf16[32,2,2048]{2,1,0:T(2,128)(2,1)} %reshape.392), calls=%async_computation.1 | async-start | bytes 524288 | tf_op jit(solution)/shard_map/while/body/eval_jaxpr/all_to_all | solution.py:66
  1151.6 7.1 collective-permute-start
  1164.4 17.6 %all-to-all-start = ((bf16[32,2,2048]{2,1,0:T(2,128)(2,1)}), bf16[32,2,2048]{2,1,0:T(2,128)(2,1)}, u32[]{:S(2)}, u32[]{:S(2)}) async-start(bf16[32,2,2048]{2,1,0:T(2,128)(2,1)} %bitcast.172), calls=%async_computation | async-start | bytes 524288 | tf_op jit(solution)/shard_map/while/body/eval_jaxpr/all_to_all | solution.py:59
  1190.3 17.1 %all-to-all-start.1 = ((bf16[32,2,2048]{2,1,0:T(2,128)(2,1)}), bf16[32,2,2048]{2,1,0:T(2,128)(2,1)S(1)}, u32[]{:S(2)}, u32[]{:S(2)}) async-start(bf16[32,2,2048]{2,1,0:T(2,128)(2,1)} %reshape.392), calls=%async_computation.1 | async-start | bytes 524288 | tf_op jit(solution)/shard_map/while/body/eval_jaxpr/all_to_all | solution.py:66
  1209.2 7.1 collective-permute-start
  1222.0 17.6 %all-to-all-start = ((bf16[32,2,2048]{2,1,0:T(2,128)(2,1)}), bf16[32,2,2048]{2,1,0:T(2,128)(2,1)}, u32[]{:S(2)}, u32[]{:S(2)}) async-start(bf16[32,2,2048]{2,1,0:T(2,128)(2,1)} %bitcast.172), calls=%async_computation | async-start | bytes 524288 | tf_op jit(solution)/shard_map/while/body/eval_jaxpr/all_to_all | solution.py:59
  1247.9 17.1 %all-to-all-start.1 = ((bf16[32,2,2048]{2,1,0:T(2,128)(2,1)}), bf16[32,2,2048]{2,1,0:T(2,128)(2,1)S(1)}, u32[]{:S(2)}, u32[]{:S(2)}) async-start(bf16[32,2,2048]{2,1,0:T(2,128)(2,1)} %reshape.392), calls=%async_computation.1 | async-start | bytes 524288 | tf_op jit(solution)/shard_map/while/body/eval_jaxpr/all_to_all | solution.py:66
  1266.9 7.1 collective-permute-start
  1280.6 17.6 %all-to-all-start.2 = ((bf16[32,2,2048]{2,1,0:T(2,128)(2,1)}), bf16[32,2,2048]{2,1,0:T(2,128)(2,1)}, u32[]{:S(2)}, u32[]{:S(2)}) async-start(bf16[32,2,2048]{2,1,0:T(2,128)(2,1)} %bitcast.183), calls=%async_computation.2 | async-start | bytes 524288 | tf_op jit(solution)/shard_map/all_to_all | solution.py:59
  1306.6 17.1 %all-to-all-start.3 = ((bf16[32,2,2048]{2,1,0:T(2,128)(2,1)}), bf16[32,2,2048]{2,1,0:T(2,128)(2,1)S(1)}, u32[]{:S(2)}, u32[]{:S(2)}) async-start(bf16[32,2,2048]{2,1,0:T(2,128)(2,1)} %reshape.316), calls=%async_computation.3 | async-start | bytes 524288 | tf_op jit(solution)/shard_map/all_to_all | solution.py:66
  (71 other events, 734.5 us)
where the time goes:
time: 1340 us; the launch traced here: 1330 us
  waiting for transfers between devices  548 us (41%)
  starting transfers between devices  341 us (25%)
  local copies, waits for them, and re-layouts  211 us (16%)
  matrix products  160 us (12%)
  other arithmetic  62.5 us (5%)
    all_to_all x23, waiting for transfers between devices, moe_layer(): lax.all_to_all(jnp.repeat(outgoing, 2, axis=0), 'expert', split_axis=0, c...  266 us
    all_to_all x23, waiting for transfers between devices, moe_layer(): lax.all_to_all(partial_out, 'expert', split_axis=0, concat_axis=0, tiled=...  241 us
    all_to_all x23, starting transfers between devices, moe_layer(): lax.all_to_all(jnp.repeat(outgoing, 2, axis=0), 'expert', split_axis=0, c...  111 us
    ppermute x22, starting transfers between devices, from_behind(): return lax.ppermute(block, axis, route)  107 us
    all_to_all x23, starting transfers between devices, moe_layer(): lax.all_to_all(partial_out, 'expert', split_axis=0, concat_axis=0, tiled=...  92.4 us
    dot_general x23, matrix products, expert_rows(): jnp.dot(hidden, down_piece, preferred_element_type=jnp.float32)  69.1 us
    dot_general x23, matrix products, expert_rows(): jnp.dot(rows_flat, gate_piece, preferred_element_type=jnp.float32)  54.6 us
    gather x115, local copies, waits for them, and re-layouts, moe_layer(): picked = jnp.take_along_axis(logits, ids_now, axis=1)  51.6 us
  transfers between devices with their start and end apart: 90, of which 90 were waited for; matrix products, arithmetic and copies ran while one was open for 7% of the time, Pallas kernels for 0%

commit v1 on v0

v1 whole, which is shorter than its diff:
```python
import functools

import jax
import jax.numpy as jnp
from jax import lax
from jax.experimental import pallas as pl
from jax.experimental.pallas import tpu as pltpu
from jax.sharding import PartitionSpec as P

CAP = 2
norm_epsilon = 1e-06

STRIDE = 1
LAG = 0

MESH = pl.DeviceIdType.MESH
LANES = 128
EXPERT_LANE = 64


def relay_kernel(
    sections,
    held,
    tokens_ref,
    mask_ref,
    choose_ref,
    router_ref,
    gain_ref,
    gate_hbm,
    up_hbm,
    down_hbm,
    out_ref,
    gate_up,
    down,
    inbox,
    stage,
    final,
    row_send,
    row_recv,
    pair_recv,
    half_send,
    half_recv,
    back_send,
    back_recv,
    stream_send,
    stream_recv,
    share_send,
    share_recv,
    weight_sem,
    inbox_send_sem,
    inbox_sem,
    stage_sem,
    final_sem,
    row_send_sem,
    row_sem,
    pair_send_sem,
    pair_sem,
    half_send_sem,
    half_sem,
    back_send_sem,
    back_sem,
    stream_send_sem,
    stream_sem,
    share_send_sem,
    share_sem,
):
    section = lax.axis_index("section")
    place = lax.axis_index("expert")
    mine = lax.div(place, 2)
    core = lax.rem(place, 2)
    following = lax.rem(section + 1, sections)
    sibling = mine * 2 + 1 - core
    rows = tokens_ref.shape[0]
    slots = held * CAP
    ff = gate_hbm.shape[2]
    near_slots = row_recv.shape[0]
    far_slots = back_recv.shape[0]
    pass_length = STRIDE * sections
    last_layer = sections - 1 + STRIDE * (2 * sections - 1)
    last_combine = sections - 1 + STRIDE * 2 * sections

    def flat(value):
        return value.reshape(slots, value.shape[-1])

    def blocks(value):
        return value.astype(jnp.bfloat16).reshape(held, CAP, value.shape[-1])

    def other(step):
        return lax.rem(mine + step, held)

    def settle(ref, sem):
        pltpu.make_async_copy(ref, ref, sem).wait()

    loads = []
    for virtual in range(2):
        loads.append(
            [
                pltpu.make_async_copy(
                    gate_hbm.at[virtual],
                    gate_up.at[virtual, :, pl.ds(0, ff)],
                    weight_sem.at[virtual, 0],
                ),
                pltpu.make_async_copy(
                    up_hbm.at[virtual],
                    gate_up.at[virtual, :, pl.ds(ff, ff)],
                    weight_sem.at[virtual, 1],
                ),
                pltpu.make_async_copy(
                    down_hbm.at[virtual], down.at[virtual], weight_sem.at[virtual, 2]
                ),
            ]
        )
        for load in loads[-1]:
            load.start()

    barrier = pltpu.get_barrier_semaphore()
    greeted = 0

    def greet(to_section, to_place):
        pl.semaphore_signal(
            barrier, inc=1, device_id=(to_section, to_place), device_id_type=MESH
        )

    for ahead in range(sections):
        to_section = lax.rem(section + ahead, sections)
        if ahead in (0, 1, sections - 1):
            first = 1 if ahead == 0 else 0

            def greet_step(step, carry, to_section=to_section):
                greet(to_section, other(step) * 2 + core)
                return carry

            lax.fori_loop(first, held, greet_step, 0)
            greeted += held - first
        else:
            greet(to_section, place)
            greeted += 1
    greet(section, sibling)
    pl.semaphore_wait(barrier, greeted + 1)

    def inbox_copy(index):
        return pltpu.make_async_remote_copy(
            tokens_ref,
            inbox.at[index],
            inbox_send_sem,
            inbox_sem.at[index],
            device_id=(0, place),
            device_id_type=MESH,
        )

    def stage_copy(index):
        return pltpu.make_async_remote_copy(
            stage.at[index],
            final,
            stage_sem.at[index],
            final_sem,
            device_id=(index, place),
            device_id_type=MESH,
        )

    @pl.when(section > 0)
    def _():
        inbox_copy(section).start()

    inbox[0] = tokens_ref[...]

    def virtual_of(step):
        return jnp.where(step - STRIDE * section >= pass_length, 1, 0)

    def home(now):
        far = lax.rem(now, far_slots)
        near = lax.rem(now, near_slots)
        two = lax.rem(now, 2)
        target = lax.rem(now + STRIDE, far_slots)

        @pl.when(now >= STRIDE)
        def _():
            settle(stream_recv.at[far], stream_sem.at[far])
            settle(share_recv.at[far], share_sem.at[far])
            settle(back_recv.at[far], back_sem.at[far])

        added = jnp.dot(
            share_recv[far][:, :slots], flat(back_recv[far]), preferred_element_type=jnp.float32
        )
        summed = stream_recv[far].astype(jnp.float32) + (added[:rows] + added[rows:])
        summed = summed.astype(jnp.bfloat16)

        @pl.when((section == 0) & (now >= 2 * pass_length))
        def _():
            index = now - 2 * pass_length

            @pl.when(index == 0)
            def _():
                final[...] = summed

            @pl.when(index > 0)
            def _():
                stage[index] = summed
                stage_copy(index).start()

        @pl.when(now <= last_layer)
        def _():
            starts = (section == 0) & (now < sections)

            @pl.when(starts & (now > 0))
            def _():
                settle(inbox.at[now], inbox_sem.at[now])

            source = jnp.where(starts, now, 0)
            current = jnp.where(starts | (now < STRIDE), inbox[source], summed)

            @pl.when(now >= 2)
            def _():
                settle(stream_send.at[two], stream_send_sem.at[two])
                settle(share_send.at[two], share_send_sem.at[two])
                settle(row_send.at[two, pl.ds(0, held - 1)], row_send_sem.at[two])

            virtual = virtual_of(now)
            offset = now - STRIDE * section - virtual * pass_length
            micro = jnp.minimum(jnp.maximum(offset, 0), sections - 1)
            table = virtual * sections + micro

            stream = current.astype(jnp.float32)
            mean_square = jnp.mean(stream * stream, axis=-1, keepdims=True)
            normed = stream * lax.rsqrt(mean_square + norm_epsilon) * gain_ref[virtual]
            normed = normed.astype(jnp.bfloat16)
            row_send[two] = blocks(
                jnp.dot(choose_ref[table], normed, preferred_element_type=jnp.float32)
            )

            def send_rows(step, carry):
                to = other(step)
                pltpu.make_async_remote_copy(
                    row_send.at[two, to],
                    row_recv.at[near, mine],
                    row_send_sem.at[two],
                    row_sem.at[near],
                    device_id=(section, to * 2 + core),
                    device_id_type=MESH,
                ).start()
                return carry

            lax.fori_loop(1, held, send_rows, 0)
            pltpu.make_async_copy(
                row_send.at[two, mine],
                row_recv.at[near, mine],
                row_sem.at[near],
            ).start()

            stream_send[two] = current
            pltpu.make_async_remote_copy(
                stream_send.at[two],
                stream_recv.at[target],
                stream_send_sem.at[two],
                stream_sem.at[target],
                device_id=(following, place),
                device_id_type=MESH,
            ).start()

            logits = jnp.dot(normed, router_ref[virtual], preferred_element_type=jnp.float32)
            scores = mask_ref[table] / (1.0 + jnp.exp(-logits))
            lane = lax.broadcasted_iota(jnp.int32, scores.shape, 1)
            total = jnp.sum(
                jnp.where(lane >= EXPERT_LANE, scores, 0.0), axis=1, keepdims=True
            )
            share = jnp.where(lane < slots, scores / total, 0.0)
            high = share.astype(jnp.bfloat16)
            low = (share - high.astype(jnp.float32)).astype(jnp.bfloat16)
            share_send[two] = jnp.concatenate([high, low], axis=0)
            pltpu.make_async_remote_copy(
                share_send.at[two],
                share_recv.at[target],
                share_send_sem.at[two],
                share_sem.at[target],
                device_id=(following, place),
                device_id_type=MESH,
            ).start()

    def serve(step):
        near = lax.rem(step, near_slots)
        two = lax.rem(step, 2)
        target = lax.rem(step + STRIDE, far_slots)
        virtual = virtual_of(step)

        settle(row_recv.at[near], row_sem.at[near])
        forward = pltpu.make_async_remote_copy(
            row_recv.at[near],
            pair_recv.at[two],
            pair_send_sem.at[two],
            pair_sem.at[two],
            device_id=(section, sibling),
            device_id_type=MESH,
        )
        forward.start()
        for early in range(2):

            @pl.when(step == early)
            def _(early=early):
                for load in loads[early]:
                    load.wait()

        forward.wait()

        given = jnp.concatenate([flat(row_recv[near]), flat(pair_recv[two])], axis=0)
        both = jnp.dot(given, gate_up[virtual], preferred_element_type=jnp.float32)
        gate_act, up_act = both[:, :ff], both[:, ff:]
        hidden = (gate_act / (1.0 + jnp.exp(-gate_act)) * up_act).astype(jnp.bfloat16)

        half_send[two] = jnp.dot(
            hidden[slots:], down[virtual], preferred_element_type=jnp.float32
        ).astype(jnp.bfloat16)
        half = pltpu.make_async_remote_copy(
            half_send.at[two],
            half_recv.at[two],
            half_send_sem.at[two],
            half_sem.at[two],
            device_id=(section, sibling),
            device_id_type=MESH,
        )
        half.start()
        own = jnp.dot(hidden[:slots], down[virtual], preferred_element_type=jnp.float32)
        own = own.astype(jnp.bfloat16).astype(jnp.float32)

        @pl.when(step >= 2)
        def _():
            settle(back_send.at[two], back_send_sem.at[two])

        half.wait()
        back_send[two] = blocks(own + half_recv[two].astype(jnp.float32))

        def send_back(turn, carry):
            to = other(turn)
            pltpu.make_async_remote_copy(
                back_send.at[two, to],
                back_recv.at[target, mine],
                back_send_sem.at[two],
                back_sem.at[target],
                device_id=(following, to * 2 + core),
                device_id_type=MESH,
            ).start()
            return carry

        lax.fori_loop(0, held, send_back, 0)

    def iteration(now, carry):
        home(now)
        if LAG:

            @pl.when((now >= LAG) & (now <= last_layer + LAG))
            def _():
                serve(now - LAG)

        else:

            @pl.when(now <= last_layer)
            def _():
                serve(now)

        return carry

    lax.fori_loop(0, last_combine + 1, iteration, 0)

    for last in range(2):
        settle(stream_send.at[last], stream_send_sem.at[last])
        settle(share_send.at[last], share_send_sem.at[last])
        settle(row_send.at[last, pl.ds(0, held - 1)], row_send_sem.at[last])
        settle(back_send.at[last], back_send_sem.at[last])

    @pl.when(section > 0)
    def _():
        settle(tokens_ref, inbox_send_sem)
        settle(final, final_sem)

    @pl.when(section == 0)
    def _():
        for index in range(1, sections):
            settle(stage.at[index], stage_sem.at[index])

    out_ref[...] = final[...]


def tables(ids, held):
    rows = ids.shape[-2]
    lane = jnp.arange(LANES, dtype=jnp.int32)
    slots = held * CAP
    meaning = jnp.where(
        lane < slots, lane // CAP, jnp.where(lane >= EXPERT_LANE, lane - EXPERT_LANE, -1)
    )
    named = jnp.any(ids[..., None] == meaning, axis=-2).astype(jnp.float32)
    row = jnp.arange(rows)
    earlier = (row[:, None] > row[None, :]).astype(jnp.float32)
    rank = jnp.sum(earlier[:, :, None] * named[:, None, :, :], axis=2)
    fits = (lane >= slots) | (rank == (lane % CAP).astype(jnp.float32))
    mask = named * fits.astype(jnp.float32)
    choose = jnp.swapaxes(mask[..., :slots], 1, 2).astype(jnp.bfloat16)
    return mask, choose


def body(tokens, expert_ids, norm_gain, router_weight, gate_weight, up_weight, down_weight):
    sections = lax.axis_size("section")
    held = lax.axis_size("expert") // 2
    rows, features = tokens.shape[1:]
    ff = gate_weight.shape[-1]
    slots = held * CAP
    experts = router_weight.shape[-1]
    mask, choose = tables(
        expert_ids[:, 0].reshape(-1, rows, expert_ids.shape[-1]), held
    )
    lane = jnp.arange(LANES, dtype=jnp.int32)
    meaning = jnp.where(
        lane < slots, lane // CAP, jnp.where(lane >= EXPERT_LANE, lane - EXPERT_LANE, -1)
    )
    spread = (jnp.arange(experts)[:, None] == meaning[None, :]).astype(jnp.bfloat16)
    router = jnp.dot(
        router_weight[:, 0], spread, preferred_element_type=jnp.float32
    ).astype(jnp.bfloat16)

    near_slots = 2 + 2 * LAG
    far_slots = STRIDE * sections - LAG + 1
    bf16 = jnp.bfloat16
    dma = pltpu.SemaphoreType.DMA
    vmem = pl.BlockSpec(memory_space=pltpu.VMEM)
    anywhere = pl.BlockSpec(memory_space=pl.ANY)
    out = pl.pallas_call(
        functools.partial(relay_kernel, sections, held),
        out_shape=jax.ShapeDtypeStruct((rows, features), bf16),
        in_specs=[vmem] * 5 + [anywhere] * 3,
        out_specs=vmem,
        scratch_shapes=[
            pltpu.VMEM((2, features, 2 * ff), bf16),
            pltpu.VMEM((2, ff, features), bf16),
            pltpu.VMEM((sections, rows, features), bf16),
            pltpu.VMEM((sections, rows, features), bf16),
            pltpu.VMEM((rows, features), bf16),
            pltpu.VMEM((2, held, CAP, features), bf16),
            pltpu.VMEM((near_slots, held, CAP, features), bf16),
            pltpu.VMEM((2, held, CAP, features), bf16),
            pltpu.VMEM((2, slots, features), bf16),
            pltpu.VMEM((2, slots, features), bf16),
            pltpu.VMEM((2, held, CAP, features), bf16),
            pltpu.VMEM((far_slots, held, CAP, features), bf16),
            pltpu.VMEM((2, rows, features), bf16),
            pltpu.VMEM((far_slots, rows, features), bf16),
            pltpu.VMEM((2, 2 * rows, LANES), bf16),
            pltpu.VMEM((far_slots, 2 * rows, LANES), bf16),
            dma((2, 3)),
            dma,
            dma((sections,)),
            dma((sections,)),
            dma,
            dma((2,)),
            dma((near_slots,)),
            dma((2,)),
            dma((2,)),
            dma((2,)),
            dma((2,)),
            dma((2,)),
            dma((far_slots,)),
            dma((2,)),
            dma((far_slots,)),
            dma((2,)),
            dma((far_slots,)),
        ],
        compiler_params=pltpu.CompilerParams(
            collective_id=0, has_side_effects=True, vmem_limit_bytes=48 << 20
        ),
        name="relay",
    )(
        tokens[0],
        mask,
        choose,
        router,
        norm_gain.reshape(2, 1, features),
        gate_weight[:, 0, 0],
        up_weight[:, 0, 0],
        down_weight[:, 0, 0],
    )
    return out[None]


def solution(mesh):
    return jax.shard_map(
        body,
        mesh=mesh,
        in_specs=(
            P("section", "expert", None),
            P(None, "section", None, "expert", None),
            P(None, "section", None),
            P(None, "section", None, None),
            P(None, "section", "expert", None, None),
            P(None, "section", "expert", None, None),
            P(None, "section", "expert", None, None),
        ),
        out_specs=P("section", "expert", None),
        check_vma=False,
    )
```

time: 1340 us -> 466 us (0.35); the launches traced: 1330 us -> 466 us
  waiting for transfers between devices: 548 us -> 0 us
  Pallas kernels: 0 us -> 459 us
  starting transfers between devices: 341 us -> 0 us
  local copies, waits for them, and re-layouts: 211 us -> 4.93 us
  matrix products: 160 us -> 0.53 us
  other arithmetic: 62.5 us -> 1.27 us
    all_to_all x46 -> x0, waiting for transfers between devices: 507 us -> none  [the longest x23 266 us: moe_layer(): lax.all_to_all(jnp.repeat(outgoing, 2, axis=0), 'expert', split_axis=0, c...]
    pallas_call x0 -> x1, Pallas kernels: none -> 459 us  [body(): pl.pallas_call(functools.partial(relay_kernel, sections, held), out_shape...]
    all_to_all x46 -> x0, starting transfers between devices: 204 us -> none  [the longest x23 111 us: moe_layer(): lax.all_to_all(jnp.repeat(outgoing, 2, axis=0), 'expert', split_axis=0, c...]
    dot_general x92 -> x1, matrix products: 160 us -> 0.53 us  [body(): jnp.dot(router_weight[:, 0], spread, preferred_element_type=jnp.float32)]
    ppermute x44 -> x0, starting transfers between devices: 137 us -> none  [the longest x22 107 us: from_behind(): return lax.ppermute(block, axis, route)]
    reshape x184 -> x0, local copies, waits for them, and re-layouts: 79.5 us -> none  [the longest x23 42.5 us: expert_rows(): return partial_out.reshape(rows_in.shape[:-1] + (down_piece.shape[1],))]
    gather x161 -> x0, local copies, waits for them, and re-layouts: 73.8 us -> none  [the longest x115 51.6 us: moe_layer(): picked = jnp.take_along_axis(logits, ids_now, axis=1)]
    ppermute x44 -> x0, waiting for transfers between devices: 41.4 us -> none  [the longest x22 28.2 us: passed_along(): lax.ppermute(value, axis, [(source, source + steps) for source in range(i...]
  transfers between devices with their start and end apart: 90 -> 0, of which waited for: 90 -> 0; matrix products, arithmetic and copies ran while one was open for 7% -> 0% of each run, Pallas kernels for 0% -> 0%
where the time goes in v1:
time: 466 us
  Pallas kernels  459 us (98%)
  local copies, waits for them, and re-layouts  4.93 us (1%)
    pallas_call x1, Pallas kernels, body(): pl.pallas_call(functools.partial(relay_kernel, sections, held), out_shape...  459 us

profile of v1, /device:TPU:26, one launch (start us, length us, event | category | flops | bytes accessed | tf_op | source)
XLA Modules:
  0.0 465.6 jit_solution(16931418969734054742)
XLA Ops:
  0.0 0.0 copy-start
  0.0 0.9 copy.33
  0.9 0.3 compare_reduce_fusion
  1.2 0.4 copy.26
  1.6 0.1 convert_element_type.32
  1.7 0.3 copy.27
  2.0 0.6 multiply_reduce_fusion
  2.7 0.4 copy.28
  3.2 0.0 copy-start.2
  3.2 0.0 copy-start.3
  3.2 0.3 or_select_fusion
  3.4 0.3 copy.30.mask_ref
  3.8 0.0 copy-done
  3.8 0.5 fusion.router_ref
  4.3 0.0 copy-done.2
  4.3 0.0 copy-done.3
  4.3 0.0 copy-start.1
  4.4 1.9 copy-done.1
  6.2 458.7 %relay.1 = bf16[16,2048]{1,0:T(8,128)(2,1)S(1)} custom-call(bf16[16,2048]{1,0:T(8,128)(2,1)S(1)} %bitcast.20, f32[16,16,128]{2,1,0:T(8,128)S(1)} %copy.30.mask_ref, bf16[16,32,16]{2,1,0:T(8,128)(2,1)S(1)} %fusion.2.choose_ref, bf16[2,2048,128]{2,1,0:T(8,128)(2,1)S(1)} %fusion.router_ref, f32[2,1,2048]{2,1,0:T(1,128)S(1)} %copy-done.3, ...), custom_call_target="tpu_custom_call" | custom-call | tf_op jit(solution)/shard_map/relay/pallas_call | solution.py:424
  465.0 0.6 copy.35
  (7 shorter events, 0.1 us)
Async XLA Ops:
  0.0 3.8 copy-start
  3.2 1.2 copy-start.2
  3.2 1.2 copy-start.3
  4.3 1.9 copy-start.1

commit v2 on v1

v2 whole, which is shorter than its diff:
```python
import functools

import jax
import jax.numpy as jnp
from jax import lax
from jax.experimental import pallas as pl
from jax.experimental.pallas import tpu as pltpu
from jax.sharding import PartitionSpec as P

CAP = 2
norm_epsilon = 1e-06

LAG = 1

MESH = pl.DeviceIdType.MESH
LANES = 128
EXPERT_LANE = 64


def relay_kernel(
    sections,
    held,
    tokens_ref,
    mask_ref,
    choose_ref,
    router_ref,
    gain_ref,
    gate_hbm,
    up_hbm,
    down_hbm,
    out_ref,
    gate_up,
    down,
    inbox,
    stage,
    final,
    row_send,
    row_recv,
    pair_recv,
    half_send,
    half_recv,
    back_send,
    back_recv,
    stream_send,
    stream_recv,
    share_send,
    share_recv,
    weight_sem,
    inbox_send_sem,
    inbox_sem,
    stage_sem,
    final_sem,
    row_send_sem,
    row_sem,
    pair_send_sem,
    pair_sem,
    half_send_sem,
    half_sem,
    back_send_sem,
    back_sem,
    stream_send_sem,
    stream_sem,
    share_send_sem,
    share_sem,
):
    section = lax.axis_index("section")
    place = lax.axis_index("expert")
    mine = lax.div(place, 2)
    core = lax.rem(place, 2)
    level, side = lax.div(mine, 2), lax.rem(mine, 2)
    levels = held // 2
    last_section = sections - 1
    is_last = section == last_section
    following = lax.rem(section + 1, sections)
    sibling = mine * 2 + 1 - core
    rows = tokens_ref.shape[0]
    slots = held * CAP
    ff = gate_hbm.shape[2]

    def flat(value):
        return value.reshape(slots, value.shape[-1])

    def blocks(value):
        return value.astype(jnp.bfloat16).reshape(held, CAP, value.shape[-1])

    farthest = sorted(
        ((up, across) for up in range(levels) for across in (1, 0)),
        key=lambda move: (-min(move[0], levels - move[0]), -move[1]),
    )

    def chip(move):
        up, across = move
        beside = 1 - side if across else side
        return lax.rem(level + up, levels) * 2 + beside

    def settle(ref, sem):
        pltpu.make_async_copy(ref, ref, sem).wait()

    loads = []
    for virtual in range(2):
        loads.append(
            [
                pltpu.make_async_copy(
                    gate_hbm.at[virtual],
                    gate_up.at[virtual, :, pl.ds(0, ff)],
                    weight_sem.at[virtual, 0],
                ),
                pltpu.make_async_copy(
                    up_hbm.at[virtual],
                    gate_up.at[virtual, :, pl.ds(ff, ff)],
                    weight_sem.at[virtual, 1],
                ),
                pltpu.make_async_copy(
                    down_hbm.at[virtual], down.at[virtual], weight_sem.at[virtual, 2]
                ),
            ]
        )
        for load in loads[-1]:
            load.start()

    barrier = pltpu.get_barrier_semaphore()
    greeted = 0

    def greet(to_section, to_place):
        pl.semaphore_signal(
            barrier, inc=1, device_id=(to_section, to_place), device_id_type=MESH
        )

    for ahead in range(sections):
        to_section = lax.rem(section + ahead, sections)
        if ahead in (0, 1, sections - 1):
            first = 1 if ahead == 0 else 0

            def greet_step(step, carry, to_section=to_section):
                greet(to_section, lax.rem(mine + step, held) * 2 + core)
                return carry

            lax.fori_loop(first, held, greet_step, 0)
            greeted += held - first
        else:
            greet(to_section, place)
            greeted += 1
    greet(section, sibling)
    pl.semaphore_wait(barrier, greeted + 1)

    def inbox_copy(index):
        return pltpu.make_async_remote_copy(
            tokens_ref,
            inbox.at[index],
            inbox_send_sem,
            inbox_sem.at[index],
            device_id=(0, place),
            device_id_type=MESH,
        )

    @pl.when(section > 0)
    def _():
        inbox_copy(section).start()

    @pl.when(section == 0)
    def _():
        inbox[0] = tokens_ref[...]

    def combined(slot):
        added = jnp.dot(
            share_recv[slot][:, :slots],
            flat(back_recv[slot]),
            preferred_element_type=jnp.float32,
        )
        summed = stream_recv[slot].astype(jnp.float32) + (added[:rows] + added[rows:])
        return summed.astype(jnp.bfloat16)

    def home(virtual, micro):
        table = virtual * sections + micro
        starts = (section == 0) & (virtual == 0)
        ends = is_last & (virtual == 1)
        target = table + jnp.where(is_last, sections, 0)

        @pl.when(starts & (micro > 0))
        def _():
            settle(inbox.at[micro], inbox_sem.at[micro])

        @pl.when(jnp.logical_not(starts))
        def _():
            settle(stream_recv.at[table], stream_sem.at[table])
            settle(share_recv.at[table], share_sem.at[table])
            settle(back_recv.at[table], back_sem.at[table])

        current = jnp.where(starts, inbox[micro], combined(table))

        stream = current.astype(jnp.float32)
        mean_square = jnp.mean(stream * stream, axis=-1, keepdims=True)
        normed = stream * lax.rsqrt(mean_square + norm_epsilon) * gain_ref[virtual]
        normed = normed.astype(jnp.bfloat16)
        row_send[table] = blocks(
            jnp.dot(choose_ref[table], normed, preferred_element_type=jnp.float32)
        )
        for move in farthest[:-1]:
            to = chip(move)
            pltpu.make_async_remote_copy(
                row_send.at[table, to],
                row_recv.at[table, mine],
                row_send_sem.at[table],
                row_sem.at[table],
                device_id=(section, to * 2 + core),
                device_id_type=MESH,
            ).start()
        pltpu.make_async_copy(
            row_send.at[table, mine], row_recv.at[table, mine], row_sem.at[table]
        ).start()

        @pl.when(ends)
        def _():
            stream_recv[target] = current

        @pl.when(jnp.logical_not(ends))
        def _():
            stream_send[table] = current
            pltpu.make_async_remote_copy(
                stream_send.at[table],
                stream_recv.at[target],
                stream_send_sem.at[table],
                stream_sem.at[target],
                device_id=(following, place),
                device_id_type=MESH,
            ).start()

        logits = jnp.dot(normed, router_ref[virtual], preferred_element_type=jnp.float32)
        scores = mask_ref[table] / (1.0 + jnp.exp(-logits))
        lane = lax.broadcasted_iota(jnp.int32, scores.shape, 1)
        total = jnp.sum(jnp.where(lane >= EXPERT_LANE, scores, 0.0), axis=1, keepdims=True)
        share = jnp.where(lane < slots, scores / total, 0.0)
        high = share.astype(jnp.bfloat16)
        low = (share - high.astype(jnp.float32)).astype(jnp.bfloat16)
        pair = jnp.concatenate([high, low], axis=0)

        @pl.when(ends)
        def _():
            share_recv[target] = pair

        @pl.when(jnp.logical_not(ends))
        def _():
            share_send[table] = pair
            pltpu.make_async_remote_copy(
                share_send.at[table],
                share_recv.at[target],
                share_send_sem.at[table],
                share_sem.at[target],
                device_id=(following, place),
                device_id_type=MESH,
            ).start()

    def serve(virtual, micro):
        table = virtual * sections + micro
        two = lax.rem(micro, 2)
        ends = is_last & (virtual == 1)
        target = table + jnp.where(is_last, sections, 0)
        to_section = jnp.where(ends, section, following)

        settle(row_recv.at[table], row_sem.at[table])
        forward = pltpu.make_async_remote_copy(
            row_recv.at[table],
            pair_recv.at[two],
            pair_send_sem.at[two],
            pair_sem.at[two],
            device_id=(section, sibling),
            device_id_type=MESH,
        )
        forward.start()
        for early in range(2):

            @pl.when((micro == 0) & (virtual == early))
            def _(early=early):
                for load in loads[early]:
                    load.wait()

        def hidden_of(given):
            both = jnp.dot(given, gate_up[virtual], preferred_element_type=jnp.float32)
            gate_act, up_act = both[:, :ff], both[:, ff:]
            return (gate_act / (1.0 + jnp.exp(-gate_act)) * up_act).astype(jnp.bfloat16)

        def partial_of(hidden):
            return jnp.dot(
                hidden, down[virtual], preferred_element_type=jnp.float32
            ).astype(jnp.bfloat16)

        own_hidden = hidden_of(flat(row_recv[table]))
        forward.wait()
        half_send[two] = partial_of(hidden_of(flat(pair_recv[two])))
        half = pltpu.make_async_remote_copy(
            half_send.at[two],
            half_recv.at[two],
            half_send_sem.at[two],
            half_sem.at[two],
            device_id=(section, sibling),
            device_id_type=MESH,
        )
        half.start()
        own = partial_of(own_hidden).astype(jnp.float32)
        half.wait()
        back_send[table] = blocks(own + half_recv[two].astype(jnp.float32))

        def back_copy(to):
            return pltpu.make_async_remote_copy(
                back_send.at[table, to],
                back_recv.at[target, mine],
                back_send_sem.at[table],
                back_sem.at[target],
                device_id=(to_section, to * 2 + core),
                device_id_type=MESH,
            )

        for move in farthest[:-1]:
            back_copy(chip(move)).start()

        @pl.when(ends)
        def _():
            pltpu.make_async_copy(
                back_send.at[table, mine], back_recv.at[target, mine], back_sem.at[target]
            ).start()

        @pl.when(jnp.logical_not(ends))
        def _():
            back_copy(mine).start()

    def stage_copy(index):
        return pltpu.make_async_remote_copy(
            stage.at[index],
            final,
            stage_sem.at[index],
            final_sem,
            device_id=(index, place),
            device_id_type=MESH,
        )

    def finish(micro):
        slot = 2 * sections + micro
        settle(back_recv.at[slot], back_sem.at[slot])
        summed = combined(slot)

        @pl.when(micro == last_section)
        def _():
            final[...] = summed

        @pl.when(micro < last_section)
        def _():
            stage[micro] = summed
            stage_copy(micro).start()

    span = sections + LAG

    def turn(index, carry):
        virtual, step = lax.div(index, span), lax.rem(index, span)

        @pl.when(step < sections)
        def _():
            home(virtual, step)

        @pl.when(step >= LAG)
        def _():
            serve(virtual, step - LAG)

        return carry

    lax.fori_loop(0, 2 * span, turn, 0)

    @pl.when(is_last)
    def _():
        def finish_step(micro, carry):
            finish(micro)
            return carry

        lax.fori_loop(0, sections, finish_step, 0)
        for index in range(sections - 1):
            settle(stage.at[index], stage_sem.at[index])

    def drain(table, carry):
        ends = is_last & (table >= sections)
        settle(row_send.at[table, pl.ds(0, held - 1)], row_send_sem.at[table])
        settle(back_send.at[table, pl.ds(0, held - 1)], back_send_sem.at[table])

        @pl.when(jnp.logical_not(ends))
        def _():
            settle(back_send.at[table, held - 1], back_send_sem.at[table])
            settle(stream_send.at[table], stream_send_sem.at[table])
            settle(share_send.at[table], share_send_sem.at[table])

        return carry

    lax.fori_loop(0, 2 * sections, drain, 0)

    @pl.when(section > 0)
    def _():
        settle(tokens_ref, inbox_send_sem)

    @pl.when(section < last_section)
    def _():
        settle(final, final_sem)

    out_ref[...] = final[...]


def tables(ids, held):
    rows = ids.shape[-2]
    lane = jnp.arange(LANES, dtype=jnp.int32)
    slots = held * CAP
    meaning = jnp.where(
        lane < slots, lane // CAP, jnp.where(lane >= EXPERT_LANE, lane - EXPERT_LANE, -1)
    )
    named = jnp.any(ids[..., None] == meaning, axis=-2).astype(jnp.float32)
    row = jnp.arange(rows)
    earlier = (row[:, None] > row[None, :]).astype(jnp.float32)
    rank = jnp.sum(earlier[:, :, None] * named[:, None, :, :], axis=2)
    fits = (lane >= slots) | (rank == (lane % CAP).astype(jnp.float32))
    mask = named * fits.astype(jnp.float32)
    choose = jnp.swapaxes(mask[..., :slots], 1, 2).astype(jnp.bfloat16)
    return mask, choose


def body(tokens, expert_ids, norm_gain, router_weight, gate_weight, up_weight, down_weight):
    sections = lax.axis_size("section")
    held = lax.axis_size("expert") // 2
    rows, features = tokens.shape[1:]
    ff = gate_weight.shape[-1]
    slots = held * CAP
    experts = router_weight.shape[-1]
    mask, choose = tables(
        expert_ids[:, 0].reshape(-1, rows, expert_ids.shape[-1]), held
    )
    lane = jnp.arange(LANES, dtype=jnp.int32)
    meaning = jnp.where(
        lane < slots, lane // CAP, jnp.where(lane >= EXPERT_LANE, lane - EXPERT_LANE, -1)
    )
    spread = (jnp.arange(experts)[:, None] == meaning[None, :]).astype(jnp.bfloat16)
    router = jnp.dot(
        router_weight[:, 0], spread, preferred_element_type=jnp.float32
    ).astype(jnp.bfloat16)

    layers, arrivals = 2 * sections, 3 * sections
    bf16 = jnp.bfloat16
    dma = pltpu.SemaphoreType.DMA
    vmem = pl.BlockSpec(memory_space=pltpu.VMEM)
    hbm = pl.BlockSpec(memory_space=pltpu.HBM)
    block = (held, CAP, features)
    out = pl.pallas_call(
        functools.partial(relay_kernel, sections, held),
        out_shape=jax.ShapeDtypeStruct((rows, features), bf16),
        in_specs=[vmem] * 5 + [hbm] * 3,
        out_specs=vmem,
        scratch_shapes=[
            pltpu.VMEM((2, features, 2 * ff), bf16),
            pltpu.VMEM((2, ff, features), bf16),
            pltpu.VMEM((sections, rows, features), bf16),
            pltpu.VMEM((sections, rows, features), bf16),
            pltpu.VMEM((rows, features), bf16),
            pltpu.VMEM((layers, *block), bf16),
            pltpu.VMEM((layers, *block), bf16),
            pltpu.VMEM((2, *block), bf16),
            pltpu.VMEM((2, slots, features), bf16),
            pltpu.VMEM((2, slots, features), bf16),
            pltpu.VMEM((layers, *block), bf16),
            pltpu.VMEM((arrivals, *block), bf16),
            pltpu.VMEM((layers, rows, features), bf16),
            pltpu.VMEM((arrivals, rows, features), bf16),
            pltpu.VMEM((layers, 2 * rows, LANES), bf16),
            pltpu.VMEM((arrivals, 2 * rows, LANES), bf16),
            dma((2, 3)),
            dma,
            dma((sections,)),
            dma((sections,)),
            dma,
            dma((layers,)),
            dma((layers,)),
            dma((2,)),
            dma((2,)),
            dma((2,)),
            dma((2,)),
            dma((layers,)),
            dma((arrivals,)),
            dma((layers,)),
            dma((arrivals,)),
            dma((layers,)),
            dma((arrivals,)),
        ],
        compiler_params=pltpu.CompilerParams(
            collective_id=0, has_side_effects=True, vmem_limit_bytes=48 << 20
        ),
        name="relay",
    )(
        tokens[0],
        mask,
        choose,
        router,
        norm_gain.reshape(2, 1, features),
        gate_weight[:, 0, 0],
        up_weight[:, 0, 0],
        down_weight[:, 0, 0],
    )
    return out[None]


def solution(mesh):
    return jax.shard_map(
        body,
        mesh=mesh,
        in_specs=(
            P("section", "expert", None),
            P(None, "section", None, "expert", None),
            P(None, "section", None),
            P(None, "section", None, None),
            P(None, "section", "expert", None, None),
            P(None, "section", "expert", None, None),
            P(None, "section", "expert", None, None),
        ),
        out_specs=P("section", "expert", None),
        check_vma=False,
    )
```

time: 466 us -> 363 us (0.78)
  Pallas kernels: 459 us -> 354 us
    pallas_call x1, Pallas kernels: 459 us -> 354 us  [body(): pl.pallas_call(functools.partial(relay_kernel, sections, held), out_shape...]
where the time goes in v2:
time: 363 us; the launch traced here: 361 us
  Pallas kernels  354 us (98%)
  local copies, waits for them, and re-layouts  4.93 us (1%)
    pallas_call x1, Pallas kernels, body(): pl.pallas_call(functools.partial(relay_kernel, sections, held), out_shape...  354 us

profile of v2, /device:TPU:26, one launch (start us, length us, event | category | flops | bytes accessed | tf_op | source)
XLA Modules:
  0.0 361.0 jit_solution(11355438439745038406)
XLA Ops:
  0.0 0.0 copy-start
  0.0 0.9 copy.33
  0.9 0.3 compare_reduce_fusion
  1.2 0.4 copy.26
  1.6 0.1 convert_element_type.32
  1.7 0.3 copy.27
  2.0 0.6 multiply_reduce_fusion
  2.7 0.4 copy.28
  3.2 0.0 copy-start.2
  3.2 0.0 copy-start.3
  3.2 0.3 or_select_fusion
  3.4 0.3 copy.30.mask_ref
  3.8 0.0 copy-done
  3.8 0.5 fusion.router_ref
  4.3 0.0 copy-done.2
  4.3 0.0 copy-done.3
  4.3 0.0 copy-start.1
  4.4 1.9 copy-done.1
  6.2 354.1 %relay.1 = bf16[16,2048]{1,0:T(8,128)(2,1)S(1)} custom-call(bf16[16,2048]{1,0:T(8,128)(2,1)S(1)} %bitcast.20, f32[16,16,128]{2,1,0:T(8,128)S(1)} %copy.30.mask_ref, bf16[16,32,16]{2,1,0:T(8,128)(2,1)S(1)} %fusion.2.choose_ref, bf16[2,2048,128]{2,1,0:T(8,128)(2,1)S(1)} %fusion.router_ref, f32[2,1,2048]{2,1,0:T(1,128)S(1)} %copy-done.3, ...), custom_call_target="tpu_custom_call" | custom-call | tf_op jit(solution)/shard_map/relay/pallas_call | solution.py:445
  360.4 0.6 copy.35
  (7 shorter events, 0.1 us)
Async XLA Ops:
  0.0 3.8 %copy-start = (bf16[2,1,2048,64]{2,3,1,0:T(8,128)(2,1)S(1)}, bf16[2,1,2048,64]{2,3,1,0:T(8,128)(2,1)}, u32[]{:S(2)}) copy-start(bf16[2,1,2048,64]{2,3,1,0:T(8,128)(2,1)} %param.10) | copy-start | bytes 1572868
  3.2 1.2 copy-start.2
  3.2 1.2 copy-start.3
  4.3 1.9 copy-start.1

commit v3 on v2

--- a/solution.py
+++ b/solution.py
@@ -10,8 +10,6 @@
 CAP = 2
 norm_epsilon = 1e-06
 
-LAG = 1
-
 MESH = pl.DeviceIdType.MESH
 LANES = 128
 EXPERT_LANE = 64
@@ -20,17 +18,23 @@
 def relay_kernel(
     sections,
     held,
+    top,
     tokens_ref,
-    mask_ref,
-    choose_ref,
-    router_ref,
-    gain_ref,
+    ids_given,
+    router_given,
+    gain_given,
     gate_hbm,
     up_hbm,
     down_hbm,
     out_ref,
     gate_up,
     down,
+    ids_ref,
+    router_packed,
+    router_ref,
+    gain_ref,
+    mask_ref,
+    choose_ref,
     inbox,
     stage,
     final,
@@ -46,6 +50,8 @@
     share_send,
     share_recv,
     weight_sem,
+    swap_send_sem,
+    swap_sem,
     inbox_send_sem,
     inbox_sem,
     stage_sem,
@@ -69,9 +75,12 @@
     core = lax.rem(place, 2)
     level, side = lax.div(mine, 2), lax.rem(mine, 2)
     levels = held // 2
+    half = sections // 2
     last_section = sections - 1
+    homed = lax.rem(section + half, sections)
+    following = lax.rem(section + 1, sections)
     is_last = section == last_section
-    following = lax.rem(section + 1, sections)
+    homes_last = homed == last_section
     sibling = mine * 2 + 1 - core
     rows = tokens_ref.shape[0]
     slots = held * CAP
@@ -128,38 +137,106 @@
 
     for ahead in range(sections):
         to_section = lax.rem(section + ahead, sections)
-        if ahead in (0, 1, sections - 1):
-            first = 1 if ahead == 0 else 0
+        if ahead in (half - 1, half, half + 1):
 
             def greet_step(step, carry, to_section=to_section):
                 greet(to_section, lax.rem(mine + step, held) * 2 + core)
                 return carry
 
-            lax.fori_loop(first, held, greet_step, 0)
-            greeted += held - first
-        else:
+            lax.fori_loop(0, held, greet_step, 0)
+            greeted += held
+        elif ahead:
             greet(to_section, place)
             greeted += 1
     greet(section, sibling)
     pl.semaphore_wait(barrier, greeted + 1)
 
-    def inbox_copy(index):
-        return pltpu.make_async_remote_copy(
+    swaps = [
+        pltpu.make_async_remote_copy(
+            source,
+            target,
+            swap_send_sem.at[index],
+            swap_sem.at[index],
+            device_id=(homed, place),
+            device_id_type=MESH,
+        )
+        for index, (source, target) in enumerate(
+            (
+                (ids_given, ids_ref),
+                (gain_given, gain_ref),
+                (router_given.at[0], router_packed.at[0]),
+                (router_given.at[1], router_packed.at[1]),
+            )
+        )
+    ]
+    swaps[0].start()
+
+    @pl.when(section != half)
+    def _():
+        pltpu.make_async_remote_copy(
             tokens_ref,
-            inbox.at[index],
+            inbox.at[section],
             inbox_send_sem,
-            inbox_sem.at[index],
-            device_id=(0, place),
+            inbox_sem.at[section],
+            device_id=(half, place),
             device_id_type=MESH,
-        )
-
-    @pl.when(section > 0)
+        ).start()
+
+    @pl.when(section == half)
     def _():
-        inbox_copy(section).start()
-
-    @pl.when(section == 0)
-    def _():
-        inbox[0] = tokens_ref[...]
+        inbox[half] = tokens_ref[...]
+
+    for swap in swaps[1:]:
+        swap.start()
+
+    lane = lax.broadcasted_iota(jnp.int32, (rows, LANES), 1)
+
+    def meaning_of(lanes):
+        chosen = lax.shift_right_logical(lanes, 1)
+        rest = jnp.where(lanes >= EXPERT_LANE, lanes - EXPERT_LANE, -1)
+        return jnp.where(lanes < slots, chosen, rest)
+
+    swaps[0].wait_recv()
+    ids = ids_ref[...]
+    meaning = meaning_of(lane)
+    named = []
+    for table in range(2 * sections):
+        found = ids[:, table * top : table * top + 1] == meaning
+        for pick in range(table * top + 1, table * top + top):
+            found = found | (ids[:, pick : pick + 1] == meaning)
+        named.append(jnp.where(found, 1.0, 0.0))
+    triangle = lax.broadcasted_iota(jnp.int32, (rows, rows), 0) > lax.broadcasted_iota(
+        jnp.int32, (rows, rows), 1
+    )
+    ranks = jnp.dot(
+        jnp.where(triangle, 1.0, 0.0).astype(jnp.bfloat16),
+        jnp.concatenate(named, axis=1).astype(jnp.bfloat16),
+        preferred_element_type=jnp.float32,
+    )
+    parity = lax.rem(lane, CAP).astype(jnp.float32)
+    for table in range(2 * sections):
+        fits = (lane >= slots) | (ranks[:, table * LANES : (table + 1) * LANES] == parity)
+        mask = jnp.where(fits, named[table], 0.0)
+        mask_ref[table] = mask
+        choose_ref[table] = jnp.transpose(mask)[:slots].astype(jnp.bfloat16)
+    swaps[1].wait_recv()
+
+    def expand_router(virtual):
+        down_lanes = lax.broadcasted_iota(jnp.int32, (LANES, LANES), 0)
+        wanted = meaning_of(lax.broadcasted_iota(jnp.int32, (LANES, LANES), 1))
+        spread = jnp.concatenate(
+            [
+                jnp.where(down_lanes == wanted, 1.0, 0.0),
+                jnp.where(down_lanes - EXPERT_LANE == wanted, 1.0, 0.0),
+            ],
+            axis=1,
+        ).astype(jnp.bfloat16)
+        wide = jnp.dot(
+            router_packed[virtual], spread, preferred_element_type=jnp.float32
+        ).astype(jnp.bfloat16)
+        depth = wide.shape[0]
+        router_ref[virtual, pl.ds(0, depth)] = wide[:, :LANES]
+        router_ref[virtual, pl.ds(depth, depth)] = wide[:, LANES:]
 
     def combined(slot):
         added = jnp.dot(
@@ -172,11 +249,11 @@
 
     def home(virtual, micro):
         table = virtual * sections + micro
-        starts = (section == 0) & (virtual == 0)
-        ends = is_last & (virtual == 1)
-        target = table + jnp.where(is_last, sections, 0)
-
-        @pl.when(starts & (micro > 0))
+        starts = (homed == 0) & (virtual == 0)
+        ends = homes_last & (virtual == 1)
+        target = table + jnp.where(homes_last, sections, 0)
+
+        @pl.when(starts & (micro != half))
         def _():
             settle(inbox.at[micro], inbox_sem.at[micro])
 
@@ -195,19 +272,16 @@
         row_send[table] = blocks(
             jnp.dot(choose_ref[table], normed, preferred_element_type=jnp.float32)
         )
-        for move in farthest[:-1]:
+        for move in farthest:
             to = chip(move)
             pltpu.make_async_remote_copy(
                 row_send.at[table, to],
                 row_recv.at[table, mine],
                 row_send_sem.at[table],
                 row_sem.at[table],
-                device_id=(section, to * 2 + core),
+                device_id=(homed, to * 2 + core),
                 device_id_type=MESH,
             ).start()
-        pltpu.make_async_copy(
-            row_send.at[table, mine], row_recv.at[table, mine], row_sem.at[table]
-        ).start()
 
         @pl.when(ends)
         def _():
@@ -225,9 +299,15 @@
                 device_id_type=MESH,
             ).start()
 
+        for first in range(2):
+
+            @pl.when((micro == 0) & (virtual == first))
+            def _(first=first):
+                swaps[2 + first].wait_recv()
+                expand_router(first)
+
         logits = jnp.dot(normed, router_ref[virtual], preferred_element_type=jnp.float32)
         scores = mask_ref[table] / (1.0 + jnp.exp(-logits))
-        lane = lax.broadcasted_iota(jnp.int32, scores.shape, 1)
         total = jnp.sum(jnp.where(lane >= EXPERT_LANE, scores, 0.0), axis=1, keepdims=True)
         share = jnp.where(lane < slots, scores / total, 0.0)
         high = share.astype(jnp.bfloat16)
@@ -253,9 +333,9 @@
     def serve(virtual, micro):
         table = virtual * sections + micro
         two = lax.rem(micro, 2)
-        ends = is_last & (virtual == 1)
         target = table + jnp.where(is_last, sections, 0)
-        to_section = jnp.where(ends, section, following)
+        to_home = lax.rem(section + 1 + half, sections)
+        to_home = jnp.where(is_last & (virtual == 1), last_section - half, to_home)
 
         settle(row_recv.at[table], row_sem.at[table])
         forward = pltpu.make_async_remote_copy(
@@ -287,7 +367,7 @@
         own_hidden = hidden_of(flat(row_recv[table]))
         forward.wait()
         half_send[two] = partial_of(hidden_of(flat(pair_recv[two])))
-        half = pltpu.make_async_remote_copy(
+        exchange = pltpu.make_async_remote_copy(
             half_send.at[two],
             half_recv.at[two],
             half_send_sem.at[two],
@@ -295,33 +375,21 @@
             device_id=(section, sibling),
             device_id_type=MESH,
         )
-        half.start()
+        exchange.start()
         own = partial_of(own_hidden).astype(jnp.float32)
-        half.wait()
+        exchange.wait()
         back_send[table] = blocks(own + half_recv[two].astype(jnp.float32))
 
-        def back_copy(to):
-            return pltpu.make_async_remote_copy(
+        for move in farthest:
+            to = chip(move)
+            pltpu.make_async_remote_copy(
                 back_send.at[table, to],
                 back_recv.at[target, mine],
                 back_send_sem.at[table],
                 back_sem.at[target],
-                device_id=(to_section, to * 2 + core),
+                device_id=(to_home, to * 2 + core),
                 device_id_type=MESH,
-            )
-
-        for move in farthest[:-1]:
-            back_copy(chip(move)).start()
-
-        @pl.when(ends)
-        def _():
-            pltpu.make_async_copy(
-                back_send.at[table, mine], back_recv.at[target, mine], back_sem.at[target]
             ).start()
-
-        @pl.when(jnp.logical_not(ends))
-        def _():
-            back_copy(mine).start()
 
     def stage_copy(index):
         return pltpu.make_async_remote_copy(
@@ -338,83 +406,73 @@
         settle(back_recv.at[slot], back_sem.at[slot])
         summed = combined(slot)
 
-        @pl.when(micro == last_section)
+        @pl.when(micro == section)
         def _():
             final[...] = summed
 
-        @pl.when(micro < last_section)
+        @pl.when(micro != section)
         def _():
             stage[micro] = summed
             stage_copy(micro).start()
 
-    span = sections + LAG
-
     def turn(index, carry):
-        virtual, step = lax.div(index, span), lax.rem(index, span)
-
-        @pl.when(step < sections)
-        def _():
-            home(virtual, step)
-
-        @pl.when(step >= LAG)
-        def _():
-            serve(virtual, step - LAG)
+        phase, micro = lax.div(index, sections), lax.rem(index, sections)
+        virtual = lax.div(phase, 2)
+        at_home = (lax.rem(phase, 2) == 0) == (section >= half)
+
+        @pl.when(at_home)
+        def _():
+            home(virtual, micro)
+
+        @pl.when(jnp.logical_not(at_home))
+        def _():
+            serve(virtual, micro)
 
         return carry
 
-    lax.fori_loop(0, 2 * span, turn, 0)
-
-    @pl.when(is_last)
+    lax.fori_loop(0, 4 * sections, turn, 0)
+
+    @pl.when(homes_last)
     def _():
         def finish_step(micro, carry):
             finish(micro)
             return carry
 
         lax.fori_loop(0, sections, finish_step, 0)
-        for index in range(sections - 1):
-            settle(stage.at[index], stage_sem.at[index])
+
+        def stage_drain(micro, carry):
+            @pl.when(micro != section)
+            def _():
+                settle(stage.at[micro], stage_sem.at[micro])
+
+            return carry
+
+        lax.fori_loop(0, sections, stage_drain, 0)
 
     def drain(table, carry):
-        ends = is_last & (table >= sections)
-        settle(row_send.at[table, pl.ds(0, held - 1)], row_send_sem.at[table])
-        settle(back_send.at[table, pl.ds(0, held - 1)], back_send_sem.at[table])
-
-        @pl.when(jnp.logical_not(ends))
-        def _():
-            settle(back_send.at[table, held - 1], back_send_sem.at[table])
+        settle(row_send.at[table], row_send_sem.at[table])
+        settle(back_send.at[table], back_send_sem.at[table])
+
+        @pl.when(jnp.logical_not(homes_last & (table >= sections)))
+        def _():
             settle(stream_send.at[table], stream_send_sem.at[table])
             settle(share_send.at[table], share_send_sem.at[table])
 
         return carry
 
     lax.fori_loop(0, 2 * sections, drain, 0)
-
-    @pl.when(section > 0)
+    for swap in swaps:
+        swap.wait_send()
+
+    @pl.when(section != half)
     def _():
         settle(tokens_ref, inbox_send_sem)
 
-    @pl.when(section < last_section)
+    @pl.when(jnp.logical_not(homes_last))
     def _():
         settle(final, final_sem)
 
     out_ref[...] = final[...]
-
-
-def tables(ids, held):
-    rows = ids.shape[-2]
-    lane = jnp.arange(LANES, dtype=jnp.int32)
-    slots = held * CAP
-    meaning = jnp.where(
-        lane < slots, lane // CAP, jnp.where(lane >= EXPERT_LANE, lane - EXPERT_LANE, -1)
-    )
-    named = jnp.any(ids[..., None] == meaning, axis=-2).astype(jnp.float32)
-    row = jnp.arange(rows)
-    earlier = (row[:, None] > row[None, :]).astype(jnp.float32)
-    rank = jnp.sum(earlier[:, :, None] * named[:, None, :, :], axis=2)
-    fits = (lane >= slots) | (rank == (lane % CAP).astype(jnp.float32))
-    mask = named * fits.astype(jnp.float32)
-    choose = jnp.swapaxes(mask[..., :slots], 1, 2).astype(jnp.bfloat16)
-    return mask, choose
 
 
 def body(tokens, expert_ids, norm_gain, router_weight, gate_weight, up_weight, down_weight):
@@ -423,18 +481,14 @@
     rows, features = tokens.shape[1:]
     ff = gate_weight.shape[-1]
     slots = held * CAP
-    experts = router_weight.shape[-1]
-    mask, choose = tables(
-        expert_ids[:, 0].reshape(-1, rows, expert_ids.shape[-1]), held
+    top = expert_ids.shape[-1]
+    ids = expert_ids[:, 0].reshape(-1, rows, top)
+    ids = jnp.swapaxes(ids, 0, 1).reshape(rows, -1)
+    ids = jnp.pad(ids, ((0, 0), (0, LANES - ids.shape[1])))
+    router = router_weight[:, 0]
+    router = jnp.concatenate(
+        [router[:, : features // 2], router[:, features // 2 :]], axis=-1
     )
-    lane = jnp.arange(LANES, dtype=jnp.int32)
-    meaning = jnp.where(
-        lane < slots, lane // CAP, jnp.where(lane >= EXPERT_LANE, lane - EXPERT_LANE, -1)
-    )
-    spread = (jnp.arange(experts)[:, None] == meaning[None, :]).astype(jnp.bfloat16)
-    router = jnp.dot(
-        router_weight[:, 0], spread, preferred_element_type=jnp.float32
-    ).astype(jnp.bfloat16)
 
     layers, arrivals = 2 * sections, 3 * sections
     bf16 = jnp.bfloat16
@@ -443,13 +497,19 @@
     hbm = pl.BlockSpec(memory_space=pltpu.HBM)
     block = (held, CAP, features)
     out = pl.pallas_call(
-        functools.partial(relay_kernel, sections, held),
+        functools.partial(relay_kernel, sections, held, top),
         out_shape=jax.ShapeDtypeStruct((rows, features), bf16),
-        in_specs=[vmem] * 5 + [hbm] * 3,
+        in_specs=[vmem] * 4 + [hbm] * 3,
         out_specs=vmem,
         scratch_shapes=[
             pltpu.VMEM((2, features, 2 * ff), bf16),
             pltpu.VMEM((2, ff, features), bf16),
+            pltpu.VMEM((rows, LANES), jnp.int32),
+            pltpu.VMEM((2, features // 2, LANES), bf16),
+            pltpu.VMEM((2, features, LANES), bf16),
+            pltpu.VMEM((2, 1, features), jnp.float32),
+            pltpu.VMEM((layers, rows, LANES), jnp.float32),
+            pltpu.VMEM((layers, slots, rows), bf16),
             pltpu.VMEM((sections, rows, features), bf16),
             pltpu.VMEM((sections, rows, features), bf16),
             pltpu.VMEM((rows, features), bf16),
@@ -465,6 +525,8 @@
             pltpu.VMEM((layers, 2 * rows, LANES), bf16),
             pltpu.VMEM((arrivals, 2 * rows, LANES), bf16),
             dma((2, 3)),
+            dma((4,)),
+            dma((4,)),
             dma,
             dma((sections,)),
             dma((sections,)),
@@ -488,8 +550,7 @@
         name="relay",
     )(
         tokens[0],
-        mask,
-        choose,
+        ids,
         router,
         norm_gain.reshape(2, 1, features),
         gate_weight[:, 0, 0],

time: 363 us -> 370 us (1.019)
  Pallas kernels: 354 us -> 364 us
    pallas_call x1, Pallas kernels: 354 us -> 364 us  [body(): pl.pallas_call(functools.partial(relay_kernel, sections, held, top), out_...]
where the time goes in v3:
time: 370 us
  Pallas kernels  364 us (98%)
  local copies, waits for them, and re-layouts  5.57 us (2%)
    pallas_call x1, Pallas kernels, body(): pl.pallas_call(functools.partial(relay_kernel, sections, held, top), out_...  364 us

profile of v3, /device:TPU:26, one launch (start us, length us, event | category | flops | bytes accessed | tf_op | source)
XLA Modules:
  0.0 370.3 jit_solution(13657934135294693558)
XLA Ops:
  0.0 0.0 copy-start.4
  0.0 0.0 copy-start.2
  0.0 0.0 copy-start
  0.0 0.0 copy-start.3
  0.0 2.5 copy.12
  2.5 1.3 fusion
  3.8 1.1 pad_maximum_fusion.router_given
  4.9 0.0 copy-done.4
  4.9 0.1 copy.11
  5.0 0.0 copy-done.2
  5.0 0.0 copy-done
  5.0 0.0 copy-done.3
  5.0 0.0 copy-start.1
  5.0 1.0 copy-done.1
  6.1 363.6 %relay.1 = bf16[16,2048]{1,0:T(8,128)(2,1)S(1)} custom-call(bf16[16,2048]{1,0:T(8,128)(2,1)S(1)} %bitcast.15, s32[16,128]{1,0:T(8,128)S(1)} %pad.4.ids_given, bf16[2,1024,128]{2,1,0:T(8,128)(2,1)S(1)} %copy-done.1, f32[2,1,2048]{2,1,0:T(1,128)S(1)} %copy-done.3, bf16[2,2048,384]{2,1,0:T(8,128)(2,1)S(1)} %bitcast.13, bf16[2,2048,384]{2,1,0:T(8,128)(2,1)} %bitcast.17, ...), custom_call_target="tpu_custom_call" | custom-call | tf_op jit(solution)/shard_map/relay/pallas_call | solution.py:499
  369.7 0.6 copy.16
  (4 shorter events, 0.0 us)
Async XLA Ops:
  0.0 4.9 %copy-start.4 = (s32[2,1,8,16,6]{3,2,4,1,0:T(8,128)S(1)}, s32[2,1,8,16,6]{3,2,4,1,0:T(8,128)}, u32[]{:S(2)}) copy-start(s32[2,1,8,16,6]{3,2,4,1,0:T(8,128)} %param.8) | copy-start | bytes 18436
  0.0 5.0 %copy-start.2 = (bf16[1,16,2048]{2,1,0:T(8,128)(2,1)S(1)}, bf16[1,16,2048]{2,1,0:T(8,128)(2,1)}, u32[]{:S(2)}) copy-start(bf16[1,16,2048]{2,1,0:T(8,128)(2,1)} %param.7) | copy-start | bytes 196612
  0.0 5.0 %copy-start = (bf16[2,1,1,2048,384]{4,3,2,1,0:T(8,128)(2,1)S(1)}, bf16[2,1,1,2048,384]{4,3,2,1,0:T(8,128)(2,1)}, u32[]{:S(2)}) copy-start(bf16[2,1,1,2048,384]{4,3,2,1,0:T(8,128)(2,1)} %param.11) | copy-start | bytes 9437188
  0.0 5.0 %copy-start.3 = (f32[2,1,2048]{2,1,0:T(1,128)S(1)}, f32[2,1,2048]{2,1,0:T(1,128)}, u32[]{:S(2)}) copy-start(f32[2,1,2048]{2,1,0:T(1,128)} %gain_given.1) | copy-start | bytes 49156
  5.0 1.0 copy-start.1

commit v4 on v3

--- a/solution.py
+++ b/solution.py
@@ -40,9 +40,6 @@
     final,
     row_send,
     row_recv,
-    pair_recv,
-    half_send,
-    half_recv,
     back_send,
     back_recv,
     stream_send,
@@ -50,6 +47,8 @@
     share_send,
     share_recv,
     weight_sem,
+    lend_sem,
+    borrow_sem,
     swap_send_sem,
     swap_sem,
     inbox_send_sem,
@@ -58,10 +57,6 @@
     final_sem,
     row_send_sem,
     row_sem,
-    pair_send_sem,
-    pair_sem,
-    half_send_sem,
-    half_sem,
     back_send_sem,
     back_sem,
     stream_send_sem,
@@ -105,27 +100,40 @@
     def settle(ref, sem):
         pltpu.make_async_copy(ref, ref, sem).wait()
 
-    loads = []
-    for virtual in range(2):
-        loads.append(
-            [
-                pltpu.make_async_copy(
-                    gate_hbm.at[virtual],
-                    gate_up.at[virtual, :, pl.ds(0, ff)],
-                    weight_sem.at[virtual, 0],
-                ),
-                pltpu.make_async_copy(
-                    up_hbm.at[virtual],
-                    gate_up.at[virtual, :, pl.ds(ff, ff)],
-                    weight_sem.at[virtual, 1],
-                ),
-                pltpu.make_async_copy(
-                    down_hbm.at[virtual], down.at[virtual], weight_sem.at[virtual, 2]
-                ),
-            ]
-        )
-        for load in loads[-1]:
-            load.start()
+    def own_half(first):
+        return pl.ds(pl.multiple_of(first + core * ff, LANES), ff)
+
+    pieces = [
+        [
+            (gate_hbm.at[virtual], gate_up.at[virtual, :, own_half(0)]),
+            (up_hbm.at[virtual], gate_up.at[virtual, :, own_half(2 * ff)]),
+            (down_hbm.at[virtual], down.at[virtual, own_half(0)]),
+        ]
+        for virtual in range(2)
+    ]
+    loads = [
+        [
+            pltpu.make_async_copy(source, target, weight_sem.at[virtual, index])
+            for index, (source, target) in enumerate(pieces[virtual])
+        ]
+        for virtual in range(2)
+    ]
+    lends = [
+        [
+            pltpu.make_async_remote_copy(
+                source,
+                target,
+                lend_sem.at[virtual, index],
+                borrow_sem.at[virtual, index],
+                device_id=(section, sibling),
+                device_id_type=MESH,
+            )
+            for index, (source, target) in enumerate(pieces[virtual])
+        ]
+        for virtual in range(2)
+    ]
+    for load in loads[0] + loads[1]:
+        load.start()
 
     barrier = pltpu.get_barrier_semaphore()
     greeted = 0
@@ -188,6 +196,9 @@
 
     for swap in swaps[1:]:
         swap.start()
+
+    for lend in lends[0] + lends[1]:
+        lend.start()
 
     lane = lax.broadcasted_iota(jnp.int32, (rows, LANES), 1)
 
@@ -332,53 +343,27 @@
 
     def serve(virtual, micro):
         table = virtual * sections + micro
-        two = lax.rem(micro, 2)
         target = table + jnp.where(is_last, sections, 0)
         to_home = lax.rem(section + 1 + half, sections)
         to_home = jnp.where(is_last & (virtual == 1), last_section - half, to_home)
 
         settle(row_recv.at[table], row_sem.at[table])
-        forward = pltpu.make_async_remote_copy(
-            row_recv.at[table],
-            pair_recv.at[two],
-            pair_send_sem.at[two],
-            pair_sem.at[two],
-            device_id=(section, sibling),
-            device_id_type=MESH,
-        )
-        forward.start()
         for early in range(2):
 
             @pl.when((micro == 0) & (virtual == early))
             def _(early=early):
-                for load in loads[early]:
+                for load, lend in zip(loads[early], lends[early]):
                     load.wait()
-
-        def hidden_of(given):
-            both = jnp.dot(given, gate_up[virtual], preferred_element_type=jnp.float32)
-            gate_act, up_act = both[:, :ff], both[:, ff:]
-            return (gate_act / (1.0 + jnp.exp(-gate_act)) * up_act).astype(jnp.bfloat16)
-
-        def partial_of(hidden):
-            return jnp.dot(
-                hidden, down[virtual], preferred_element_type=jnp.float32
-            ).astype(jnp.bfloat16)
-
-        own_hidden = hidden_of(flat(row_recv[table]))
-        forward.wait()
-        half_send[two] = partial_of(hidden_of(flat(pair_recv[two])))
-        exchange = pltpu.make_async_remote_copy(
-            half_send.at[two],
-            half_recv.at[two],
-            half_send_sem.at[two],
-            half_sem.at[two],
-            device_id=(section, sibling),
-            device_id_type=MESH,
-        )
-        exchange.start()
-        own = partial_of(own_hidden).astype(jnp.float32)
-        exchange.wait()
-        back_send[table] = blocks(own + half_recv[two].astype(jnp.float32))
+                    lend.wait_recv()
+
+        both = jnp.dot(
+            flat(row_recv[table]), gate_up[virtual], preferred_element_type=jnp.float32
+        )
+        gate_act, up_act = both[:, : 2 * ff], both[:, 2 * ff :]
+        hidden = (gate_act / (1.0 + jnp.exp(-gate_act)) * up_act).astype(jnp.bfloat16)
+        back_send[table] = blocks(
+            jnp.dot(hidden, down[virtual], preferred_element_type=jnp.float32)
+        )
 
         for move in farthest:
             to = chip(move)
@@ -471,6 +456,9 @@
     @pl.when(jnp.logical_not(homes_last))
     def _():
         settle(final, final_sem)
+
+    for lend in lends[0] + lends[1]:
+        lend.wait_send()
 
     out_ref[...] = final[...]
 
@@ -502,8 +490,8 @@
         in_specs=[vmem] * 4 + [hbm] * 3,
         out_specs=vmem,
         scratch_shapes=[
-            pltpu.VMEM((2, features, 2 * ff), bf16),
-            pltpu.VMEM((2, ff, features), bf16),
+            pltpu.VMEM((2, features, 4 * ff), bf16),
+            pltpu.VMEM((2, 2 * ff, features), bf16),
             pltpu.VMEM((rows, LANES), jnp.int32),
             pltpu.VMEM((2, features // 2, LANES), bf16),
             pltpu.VMEM((2, features, LANES), bf16),
@@ -515,15 +503,14 @@
             pltpu.VMEM((rows, features), bf16),
             pltpu.VMEM((layers, *block), bf16),
             pltpu.VMEM((layers, *block), bf16),
-            pltpu.VMEM((2, *block), bf16),
-            pltpu.VMEM((2, slots, features), bf16),
-            pltpu.VMEM((2, slots, features), bf16),
             pltpu.VMEM((layers, *block), bf16),
             pltpu.VMEM((arrivals, *block), bf16),
             pltpu.VMEM((layers, rows, features), bf16),
             pltpu.VMEM((arrivals, rows, features), bf16),
             pltpu.VMEM((layers, 2 * rows, LANES), bf16),
             pltpu.VMEM((arrivals, 2 * rows, LANES), bf16),
+            dma((2, 3)),
+            dma((2, 3)),
             dma((2, 3)),
             dma((4,)),
             dma((4,)),
@@ -533,10 +520,6 @@
             dma,
             dma((layers,)),
             dma((layers,)),
-            dma((2,)),
-            dma((2,)),
-            dma((2,)),
-            dma((2,)),
             dma((layers,)),
             dma((arrivals,)),
             dma((layers,)),
@@ -545,7 +528,7 @@
             dma((arrivals,)),
         ],
         compiler_params=pltpu.CompilerParams(
-            collective_id=0, has_side_effects=True, vmem_limit_bytes=48 << 20
+            collective_id=0, has_side_effects=True, vmem_limit_bytes=60 << 20
         ),
         name="relay",
     )(

time: 370 us -> 310 us (0.84)
  Pallas kernels: 364 us -> 305 us
    pallas_call x1, Pallas kernels: 364 us -> 305 us  [body(): pl.pallas_call(functools.partial(relay_kernel, sections, held, top), out_...]
where the time goes in v4:
time: 310 us
  Pallas kernels  305 us (98%)
  local copies, waits for them, and re-layouts  3.78 us (1%)
    pallas_call x1, Pallas kernels, body(): pl.pallas_call(functools.partial(relay_kernel, sections, held, top), out_...  305 us

profile of v4, /device:TPU:26, one launch (start us, length us, event | category | flops | bytes accessed | tf_op | source)
XLA Modules:
  0.0 309.8 jit_solution(7192775861774660088)
XLA Ops:
  0.0 0.0 copy-start
  0.0 1.5 copy.12
  1.5 0.1 fusion
  1.6 1.1 pad_maximum_fusion.router_given
  2.7 0.0 copy-done
  2.7 0.1 copy.11
  2.8 0.6 pad.4.ids_given
  3.4 304.9 %relay.1 = bf16[16,2048]{1,0:T(8,128)(2,1)} custom-call(bf16[16,2048]{1,0:T(8,128)(2,1)} %bitcast.19, s32[16,128]{1,0:T(8,128)} %pad.4.ids_given, bf16[2,1024,128]{2,1,0:T(8,128)(2,1)} %pad_maximum_fusion.router_given, f32[2,1,2048]{2,1,0:T(1,128)} %gain_given.1, bf16[2,2048,384]{2,1,0:T(8,128)(2,1)} %bitcast.14, bf16[2,2048,384]{2,1,0:T(8,128)(2,1)} %bitcast.15, ...), custom_call_target="tpu_custom_call" | custom-call | tf_op jit(solution)/shard_map/relay/pallas_call | solution.py:487
  308.3 1.5 copy.16
  (3 shorter events, 0.0 us)
Async XLA Ops:
  0.0 2.7 copy-start

commit v5 on v4

--- a/solution.py
+++ b/solution.py
@@ -132,7 +132,7 @@
         ]
         for virtual in range(2)
     ]
-    for load in loads[0] + loads[1]:
+    for load in loads[0]:
         load.start()
 
     barrier = pltpu.get_barrier_semaphore()
@@ -143,21 +143,21 @@
             barrier, inc=1, device_id=(to_section, to_place), device_id_type=MESH
         )
 
-    for ahead in range(sections):
-        to_section = lax.rem(section + ahead, sections)
-        if ahead in (half - 1, half, half + 1):
-
-            def greet_step(step, carry, to_section=to_section):
-                greet(to_section, lax.rem(mine + step, held) * 2 + core)
-                return carry
-
-            lax.fori_loop(0, held, greet_step, 0)
-            greeted += held
-        elif ahead:
-            greet(to_section, place)
-            greeted += 1
+    for ahead in range(1, sections):
+        greet(lax.rem(section + ahead, sections), place)
+        greeted += 1
     greet(section, sibling)
-    pl.semaphore_wait(barrier, greeted + 1)
+    greeted += 1
+
+    @pl.when(section == 0)
+    def _():
+        def greet_step(step, carry):
+            greet(half, lax.rem(mine + step, held) * 2 + core)
+            return carry
+
+        lax.fori_loop(1, held, greet_step, 0)
+
+    pl.semaphore_wait(barrier, jnp.where(section == half, greeted + held - 1, greeted))
 
     swaps = [
         pltpu.make_async_remote_copy(
@@ -197,8 +197,10 @@
     for swap in swaps[1:]:
         swap.start()
 
-    for lend in lends[0] + lends[1]:
-        lend.start()
+    @pl.when(section < half)
+    def _():
+        for lend in lends[0]:
+            lend.start()
 
     lane = lax.broadcasted_iota(jnp.int32, (rows, LANES), 1)
 
@@ -233,21 +235,14 @@
     swaps[1].wait_recv()
 
     def expand_router(virtual):
-        down_lanes = lax.broadcasted_iota(jnp.int32, (LANES, LANES), 0)
-        wanted = meaning_of(lax.broadcasted_iota(jnp.int32, (LANES, LANES), 1))
-        spread = jnp.concatenate(
-            [
-                jnp.where(down_lanes == wanted, 1.0, 0.0),
-                jnp.where(down_lanes - EXPERT_LANE == wanted, 1.0, 0.0),
-            ],
-            axis=1,
+        experts = router_packed.shape[1]
+        wanted = meaning_of(lax.broadcasted_iota(jnp.int32, (LANES, experts), 0))
+        spread = lax.broadcasted_iota(jnp.int32, (LANES, experts), 1) == wanted
+        router_ref[virtual] = jnp.dot(
+            jnp.where(spread, 1.0, 0.0).astype(jnp.bfloat16),
+            router_packed[virtual],
+            preferred_element_type=jnp.float32,
         ).astype(jnp.bfloat16)
-        wide = jnp.dot(
-            router_packed[virtual], spread, preferred_element_type=jnp.float32
-        ).astype(jnp.bfloat16)
-        depth = wide.shape[0]
-        router_ref[virtual, pl.ds(0, depth)] = wide[:, :LANES]
-        router_ref[virtual, pl.ds(depth, depth)] = wide[:, LANES:]
 
     def combined(slot):
         added = jnp.dot(
@@ -317,7 +312,12 @@
                 swaps[2 + first].wait_recv()
                 expand_router(first)
 
-        logits = jnp.dot(normed, router_ref[virtual], preferred_element_type=jnp.float32)
+        logits = lax.dot_general(
+            normed,
+            router_ref[virtual],
+            (((1,), (1,)), ((), ())),
+            preferred_element_type=jnp.float32,
+        )
         scores = mask_ref[table] / (1.0 + jnp.exp(-logits))
         total = jnp.sum(jnp.where(lane >= EXPERT_LANE, scores, 0.0), axis=1, keepdims=True)
         share = jnp.where(lane < slots, scores / total, 0.0)
@@ -348,19 +348,22 @@
         to_home = jnp.where(is_last & (virtual == 1), last_section - half, to_home)
 
         settle(row_recv.at[table], row_sem.at[table])
-        for early in range(2):
-
-            @pl.when((micro == 0) & (virtual == early))
-            def _(early=early):
-                for load, lend in zip(loads[early], lends[early]):
-                    load.wait()
-                    lend.wait_recv()
-
+        def arrive(pieces_used):
+            for early in range(2):
+
+                @pl.when((micro == 0) & (virtual == early))
+                def _(early=early):
+                    for index in pieces_used:
+                        loads[early][index].wait()
+                        lends[early][index].wait_recv()
+
+        arrive((0, 1))
         both = jnp.dot(
             flat(row_recv[table]), gate_up[virtual], preferred_element_type=jnp.float32
         )
         gate_act, up_act = both[:, : 2 * ff], both[:, 2 * ff :]
         hidden = (gate_act / (1.0 + jnp.exp(-gate_act)) * up_act).astype(jnp.bfloat16)
+        arrive((2,))
         back_send[table] = blocks(
             jnp.dot(hidden, down[virtual], preferred_element_type=jnp.float32)
         )
@@ -405,9 +408,20 @@
         virtual = lax.div(phase, 2)
         at_home = (lax.rem(phase, 2) == 0) == (section >= half)
 
+        @pl.when(index == sections)
+        def _():
+            for load, lend in zip(loads[1], lends[1]):
+                load.start()
+                lend.start()
+
         @pl.when(at_home)
         def _():
             home(virtual, micro)
+
+            @pl.when((section >= half) & (index == 0))
+            def _():
+                for lend in lends[0]:
+                    lend.start()
 
         @pl.when(jnp.logical_not(at_home))
         def _():
@@ -473,10 +487,7 @@
     ids = expert_ids[:, 0].reshape(-1, rows, top)
     ids = jnp.swapaxes(ids, 0, 1).reshape(rows, -1)
     ids = jnp.pad(ids, ((0, 0), (0, LANES - ids.shape[1])))
-    router = router_weight[:, 0]
-    router = jnp.concatenate(
-        [router[:, : features // 2], router[:, features // 2 :]], axis=-1
-    )
+    router = jnp.swapaxes(router_weight[:, 0], 1, 2)
 
     layers, arrivals = 2 * sections, 3 * sections
     bf16 = jnp.bfloat16
@@ -493,8 +504,8 @@
             pltpu.VMEM((2, features, 4 * ff), bf16),
             pltpu.VMEM((2, 2 * ff, features), bf16),
             pltpu.VMEM((rows, LANES), jnp.int32),
-            pltpu.VMEM((2, features // 2, LANES), bf16),
-            pltpu.VMEM((2, features, LANES), bf16),
+            pltpu.VMEM((2, router.shape[1], features), bf16),
+            pltpu.VMEM((2, LANES, features), bf16),
             pltpu.VMEM((2, 1, features), jnp.float32),
             pltpu.VMEM((layers, rows, LANES), jnp.float32),
             pltpu.VMEM((layers, slots, rows), bf16),

time: 310 us -> 299 us (0.965)
  Pallas kernels: 305 us -> 296 us
    pallas_call x1, Pallas kernels: 305 us -> 296 us  [body(): pl.pallas_call(functools.partial(relay_kernel, sections, held, top), out_...]
where the time goes in v5:
time: 299 us
  Pallas kernels  296 us (99%)
    pallas_call x1, Pallas kernels, body(): pl.pallas_call(functools.partial(relay_kernel, sections, held, top), out_...  296 us

profile of v5, /device:TPU:26, one launch (start us, length us, event | category | flops | bytes accessed | tf_op | source)
XLA Modules:
  0.0 299.1 jit_solution(14391548127011541571)
XLA Ops:
  0.0 0.8 copy.12
  0.8 0.1 copy.10
  0.9 0.6 pad.4.ids_given
  1.5 296.1 %relay.1 = bf16[16,2048]{1,0:T(8,128)(2,1)} custom-call(bf16[16,2048]{1,0:T(8,128)(2,1)} %bitcast.21, s32[16,128]{1,0:T(8,128)} %pad.4.ids_given, bf16[2,64,2048]{2,1,0:T(8,128)(2,1)} %bitcast.18, f32[2,1,2048]{2,1,0:T(1,128)} %gain_given.1, bf16[2,2048,384]{2,1,0:T(8,128)(2,1)} %bitcast.15, bf16[2,2048,384]{2,1,0:T(8,128)(2,1)} %bitcast.16, ...), custom_call_target="tpu_custom_call" | custom-call | tf_op jit(solution)/shard_map/relay/pallas_call | solution.py:498
  297.7 1.5 copy.14
  (2 shorter events, 0.0 us)

commit v6 on v5

--- a/solution.py
+++ b/solution.py
@@ -278,6 +278,10 @@
         row_send[table] = blocks(
             jnp.dot(choose_ref[table], normed, preferred_element_type=jnp.float32)
         )
+        @pl.when(starts & (micro > 0))
+        def _():
+            settle(row_send.at[table - 1], row_send_sem.at[table - 1])
+
         for move in farthest:
             to = chip(move)
             pltpu.make_async_remote_copy(
@@ -449,7 +453,10 @@
         lax.fori_loop(0, sections, stage_drain, 0)
 
     def drain(table, carry):
-        settle(row_send.at[table], row_send_sem.at[table])
+        @pl.when((homed > 0) | (table >= sections - 1))
+        def _():
+            settle(row_send.at[table], row_send_sem.at[table])
+
         settle(back_send.at[table], back_send_sem.at[table])
 
         @pl.when(jnp.logical_not(homes_last & (table >= sections)))

time: 299 us -> 294 us (0.983)
  Pallas kernels: 296 us -> 291 us
    pallas_call x1, Pallas kernels: 296 us -> 291 us  [body(): pl.pallas_call(functools.partial(relay_kernel, sections, held, top), out_...]
where the time goes in v6:
time: 294 us
  Pallas kernels  291 us (99%)
  local copies, waits for them, and re-layouts  2.98 us (1%)
    pallas_call x1, Pallas kernels, body(): pl.pallas_call(functools.partial(relay_kernel, sections, held, top), out_...  291 us

profile of v6, /device:TPU:26, one launch (start us, length us, event | category | flops | bytes accessed | tf_op | source)
XLA Modules:
  0.0 293.7 jit_solution(1976936813089434218)
XLA Ops:
  0.0 0.8 copy.12
  0.8 0.1 copy.10
  0.9 0.6 pad.4.ids_given
  1.5 290.7 %relay.1 = bf16[16,2048]{1,0:T(8,128)(2,1)} custom-call(bf16[16,2048]{1,0:T(8,128)(2,1)} %bitcast.21, s32[16,128]{1,0:T(8,128)} %pad.4.ids_given, bf16[2,64,2048]{2,1,0:T(8,128)(2,1)} %bitcast.18, f32[2,1,2048]{2,1,0:T(1,128)} %gain_given.1, bf16[2,2048,384]{2,1,0:T(8,128)(2,1)} %bitcast.15, bf16[2,2048,384]{2,1,0:T(8,128)(2,1)} %bitcast.16, ...), custom_call_target="tpu_custom_call" | custom-call | tf_op jit(solution)/shard_map/relay/pallas_call | solution.py:505
  292.2 1.5 copy.14
  (2 shorter events, 0.0 us)

commit v7 on v6

--- a/solution.py
+++ b/solution.py
@@ -293,21 +293,16 @@
                 device_id_type=MESH,
             ).start()
 
-        @pl.when(ends)
-        def _():
-            stream_recv[target] = current
-
-        @pl.when(jnp.logical_not(ends))
-        def _():
-            stream_send[table] = current
-            pltpu.make_async_remote_copy(
-                stream_send.at[table],
-                stream_recv.at[target],
-                stream_send_sem.at[table],
-                stream_sem.at[target],
-                device_id=(following, place),
-                device_id_type=MESH,
-            ).start()
+        beyond = jnp.where(ends, homed, following)
+        stream_send[table] = current
+        pltpu.make_async_remote_copy(
+            stream_send.at[table],
+            stream_recv.at[target],
+            stream_send_sem.at[table],
+            stream_sem.at[target],
+            device_id=(beyond, place),
+            device_id_type=MESH,
+        ).start()
 
         for first in range(2):
 
@@ -327,29 +322,22 @@
         share = jnp.where(lane < slots, scores / total, 0.0)
         high = share.astype(jnp.bfloat16)
         low = (share - high.astype(jnp.float32)).astype(jnp.bfloat16)
-        pair = jnp.concatenate([high, low], axis=0)
-
-        @pl.when(ends)
-        def _():
-            share_recv[target] = pair
-
-        @pl.when(jnp.logical_not(ends))
-        def _():
-            share_send[table] = pair
-            pltpu.make_async_remote_copy(
-                share_send.at[table],
-                share_recv.at[target],
-                share_send_sem.at[table],
-                share_sem.at[target],
-                device_id=(following, place),
-                device_id_type=MESH,
-            ).start()
+        share_send[table] = jnp.concatenate([high, low], axis=0)
+        pltpu.make_async_remote_copy(
+            share_send.at[table],
+            share_recv.at[target],
+            share_send_sem.at[table],
+            share_sem.at[target],
+            device_id=(beyond, place),
+            device_id_type=MESH,
+        ).start()
 
     def serve(virtual, micro):
         table = virtual * sections + micro
         target = table + jnp.where(is_last, sections, 0)
         to_home = lax.rem(section + 1 + half, sections)
-        to_home = jnp.where(is_last & (virtual == 1), last_section - half, to_home)
+        ends = is_last & (virtual == 1)
+        to_home = jnp.where(ends, section, to_home)
 
         settle(row_recv.at[table], row_sem.at[table])
         def arrive(pieces_used):
@@ -372,16 +360,28 @@
             jnp.dot(hidden, down[virtual], preferred_element_type=jnp.float32)
         )
 
-        for move in farthest:
-            to = chip(move)
-            pltpu.make_async_remote_copy(
+        def back_copy(to):
+            return pltpu.make_async_remote_copy(
                 back_send.at[table, to],
                 back_recv.at[target, mine],
                 back_send_sem.at[table],
                 back_sem.at[target],
                 device_id=(to_home, to * 2 + core),
                 device_id_type=MESH,
+            )
+
+        for move in farthest[:-1]:
+            back_copy(chip(move)).start()
+
+        @pl.when(ends)
+        def _():
+            pltpu.make_async_copy(
+                back_send.at[table, mine], back_recv.at[target, mine], back_sem.at[target]
             ).start()
+
+        @pl.when(jnp.logical_not(ends))
+        def _():
+            back_copy(mine).start()
 
     def stage_copy(index):
         return pltpu.make_async_remote_copy(
@@ -395,6 +395,8 @@
 
     def finish(micro):
         slot = 2 * sections + micro
+        settle(stream_recv.at[slot], stream_sem.at[slot])
+        settle(share_recv.at[slot], share_sem.at[slot])
         settle(back_recv.at[slot], back_sem.at[slot])
         summed = combined(slot)
 
@@ -435,7 +437,7 @@
 
     lax.fori_loop(0, 4 * sections, turn, 0)
 
-    @pl.when(homes_last)
+    @pl.when(is_last)
     def _():
         def finish_step(micro, carry):
             finish(micro)
@@ -457,12 +459,13 @@
         def _():
             settle(row_send.at[table], row_send_sem.at[table])
 
-        settle(back_send.at[table], back_send_sem.at[table])
-
-        @pl.when(jnp.logical_not(homes_last & (table >= sections)))
-        def _():
-            settle(stream_send.at[table], stream_send_sem.at[table])
-            settle(share_send.at[table], share_send_sem.at[table])
+        settle(back_send.at[table, pl.ds(0, held - 1)], back_send_sem.at[table])
+        settle(stream_send.at[table], stream_send_sem.at[table])
+        settle(share_send.at[table], share_send_sem.at[table])
+
+        @pl.when(jnp.logical_not(is_last & (table >= sections)))
+        def _():
+            settle(back_send.at[table, held - 1], back_send_sem.at[table])
 
         return carry
 
@@ -474,7 +477,7 @@
     def _():
         settle(tokens_ref, inbox_send_sem)
 
-    @pl.when(jnp.logical_not(homes_last))
+    @pl.when(jnp.logical_not(is_last))
     def _():
         settle(final, final_sem)
 

time: 294 us -> 292 us (level)
  Pallas kernels: 291 us -> 287 us
    pallas_call x1, Pallas kernels: 291 us -> 287 us  [body(): pl.pallas_call(functools.partial(relay_kernel, sections, held, top), out_...]
where the time goes in v7:
time: 292 us; the launch traced here: 290 us
  Pallas kernels  287 us (98%)
  local copies, waits for them, and re-layouts  2.98 us (1%)
    pallas_call x1, Pallas kernels, body(): pl.pallas_call(functools.partial(relay_kernel, sections, held, top), out_...  287 us

profile of v7, /device:TPU:26, one launch (start us, length us, event | category | flops | bytes accessed | tf_op | source)
XLA Modules:
  0.0 290.2 jit_solution(8252877603940729843)
XLA Ops:
  0.0 0.8 copy.12
  0.8 0.1 copy.10
  0.9 0.6 pad.4.ids_given
  1.5 287.2 %relay.1 = bf16[16,2048]{1,0:T(8,128)(2,1)} custom-call(bf16[16,2048]{1,0:T(8,128)(2,1)} %bitcast.21, s32[16,128]{1,0:T(8,128)} %pad.4.ids_given, bf16[2,64,2048]{2,1,0:T(8,128)(2,1)} %bitcast.18, f32[2,1,2048]{2,1,0:T(1,128)} %gain_given.1, bf16[2,2048,384]{2,1,0:T(8,128)(2,1)} %bitcast.15, bf16[2,2048,384]{2,1,0:T(8,128)(2,1)} %bitcast.16, ...), custom_call_target="tpu_custom_call" | custom-call | tf_op jit(solution)/shard_map/relay/pallas_call | solution.py:508
  288.8 1.5 copy.14
  (2 shorter events, 0.0 us)
